TPU v7x, 512 devices: a whole 4x8x8 slice. The times are simulated.
512 devices in a mesh: row: 32 (over x_hi, z, core), col: 16 (over y, x_lo).
Axes of the slice: x: 4 (x_hi: 2, x_lo: 2; x = x_hi * 2 + x_lo), y: 8, z: 8, core: 2. Of those that a mesh axis runs over, the one named last changes fastest.
Arguments:
- pre_silu: bfloat16 [8, 96, 96, 256], P(None, 'row', 'col'), may hold values from -6 to 6
- out_grad: bfloat16 [8, 96, 96, 256], P(None, 'row', 'col'), may hold values from -6 to 6
- query_heads: bfloat16 [32, 9216, 64], P('col', 'row'), may hold values from -10 to 10
- key_heads: bfloat16 [32, 9216, 64], P('col', 'row'), may hold values from -10 to 10
- value_heads: bfloat16 [32, 9216, 64], P('col', 'row'), may hold values from -6 to 6
- conv_weight: bfloat16 [3, 3, 256, 256], replicated, may hold values from -0.125 to 0.125
- out_weight: bfloat16 [256, 256], replicated, may hold values from -0.375 to 0.375
- input_weight: bfloat16 [256, 768], replicated, may hold values from -0.375 to 0.375
Outputs:
- grad_input: bfloat16 [8, 96, 96, 256], P(None, 'row', 'col')
All inputs are finite; a program needn't handle non-finite values.
Results may differ from a plain program's by a relative error of at most 0.0095.
Values may be sent and summed in bfloat16 or wider, within the bound.
A program may use at most 64 MiB of HBM per device.

v0:
```python
import jax
import jax.numpy as jnp
from jax import lax
from jax.sharding import PartitionSpec as P

HEADS = 4


def with_halo(cells, sides, width):
    for axis, dim in sides:
        count = lax.axis_size(axis)
        ends = count - 1
        head = lax.slice_in_dim(cells, 0, width, axis=dim)
        tail = lax.slice_in_dim(cells, cells.shape[dim] - width, cells.shape[dim], axis=dim)
        cells = jnp.concatenate(
            [
                lax.ppermute(tail, axis, [(i, (i + 1) % count) for i in range(ends)]),
                cells,
                lax.ppermute(head, axis, [((i + 1) % count, i) for i in range(ends)]),
            ],
            axis=dim,
        )
    return cells


def run_blocks(update, running, arrays, block_rows):
    amount = arrays[0].shape[1]
    grouped = tuple(
        (
            jnp.moveaxis(
                member.reshape(
                    (member.shape[0], amount // block_rows, block_rows) + member.shape[2:]
                ),
                1,
                0,
            )
            for member in arrays
        )
    )

    def advance(current, sliced):
        return (update(current, *sliced), None)

    running, unused = lax.scan(advance, running, grouped)
    return running


def contract(left, right):
    return jnp.einsum("ptd,pud->ptu", left, right, preferred_element_type=jnp.float32)


def shards(
    pre_silu, out_grad, query_heads, key_heads, value_heads, conv_weight, out_weight, input_weight
):
    samples, rows_dev, cols_dev, channels = pre_silu.shape
    head_count = HEADS
    pairs = query_heads.shape[0]
    head_dim = query_heads.shape[2]
    factor = head_dim ** (-0.5)
    padded = with_halo(out_grad, (("row", 1), ("col", 2)), 1)
    conv_sum = jnp.zeros((samples, rows_dev, cols_dev, channels), jnp.float32)
    for shift_r in (-1, 0, 1):
        for shift_c in (-1, 0, 1):
            window = padded[
                :, 1 - shift_r : 1 - shift_r + rows_dev, 1 - shift_c : 1 - shift_c + cols_dev, :
            ]
            conv_sum = conv_sum + jnp.einsum(
                "srcd,ed->srce",
                window,
                conv_weight[shift_r + 1, shift_c + 1],
                preferred_element_type=jnp.float32,
            )
    z_float = pre_silu.astype(jnp.float32)
    sigmoid_z = jax.nn.sigmoid(z_float)
    grad_z = (conv_sum * sigmoid_z * (1.0 + z_float * (1.0 - sigmoid_z))).astype(jnp.bfloat16)
    grad_attn = jnp.einsum(
        "srcd,hed->shrce",
        grad_z,
        out_weight.reshape(head_count, head_dim, channels),
        preferred_element_type=jnp.float32,
    ).astype(jnp.bfloat16)
    grad_attn = grad_attn.reshape(samples * head_count, rows_dev, cols_dev, head_dim)
    strip_heads = lax.all_to_all(grad_attn, "col", split_axis=0, concat_axis=2, tiled=True)
    width_all = strip_heads.shape[2]
    strip_rows = rows_dev * width_all
    grad_out = strip_heads.reshape(pairs, strip_rows, head_dim)
    block_rows = 4 * strip_rows

    def stats_update(running, key_block, value_block):
        running_max, norm_sum, weighted = running
        scores = contract(query_heads, key_block) * factor
        grad_probs = contract(grad_out, value_block)
        new_max = jnp.maximum(running_max, jnp.max(scores, axis=2))
        exp_scores = jnp.exp(scores - new_max[:, :, None])
        rescale = jnp.exp(running_max - new_max)
        return (
            new_max,
            norm_sum * rescale + jnp.sum(exp_scores, axis=2),
            weighted * rescale + jnp.sum(exp_scores * grad_probs, axis=2),
        )

    zero_vec = jnp.zeros((pairs, strip_rows), jnp.float32)
    init_stats = (jnp.full((pairs, strip_rows), -jnp.inf, jnp.float32), zero_vec, zero_vec)
    keys_all, values_all = (
        lax.all_gather(key_heads, "row", axis=1, tiled=True),
        lax.all_gather(value_heads, "row", axis=1, tiled=True),
    )
    stats = run_blocks(stats_update, init_stats, (keys_all, values_all), block_rows)
    log_norm = stats[0] + jnp.log(stats[1])
    row_dot = stats[2] / stats[1]

    def query_update(grad_query, key_block, value_block):
        scores = contract(query_heads, key_block) * factor
        prob_block = jnp.exp(scores - log_norm[:, :, None])
        grad_probs = contract(grad_out, value_block)
        grad_scores = (prob_block * (grad_probs - row_dot[:, :, None])).astype(jnp.bfloat16)
        return (
            grad_query
            + jnp.einsum("ptu,pud->ptd", grad_scores, key_block, preferred_element_type=jnp.float32)
            * factor
        )

    zero_rows = jnp.zeros((pairs, strip_rows, head_dim), jnp.float32)
    grad_query = run_blocks(query_update, zero_rows, (keys_all, values_all), block_rows)
    log_all, dot_all = (
        lax.all_gather(log_norm, "row", axis=1, tiled=True),
        lax.all_gather(row_dot, "row", axis=1, tiled=True),
    )

    def pair_update(running, query_block, grad_block, log_block, dot_block):
        grad_key, grad_value = running
        scores = contract(key_heads, query_block) * factor
        prob_block = jnp.exp(scores - log_block[:, None, :])
        grad_probs = contract(value_heads, grad_block)
        grad_scores = (prob_block * (grad_probs - dot_block[:, None, :])).astype(jnp.bfloat16)
        grad_key = (
            grad_key
            + jnp.einsum(
                "ptu,pud->ptd", grad_scores, query_block, preferred_element_type=jnp.float32
            )
            * factor
        )
        grad_value = grad_value + jnp.einsum(
            "ptu,pud->ptd",
            prob_block.astype(jnp.bfloat16),
            grad_block,
            preferred_element_type=jnp.float32,
        )
        return (grad_key, grad_value)

    query_block = lax.all_gather(query_heads, "row", axis=1, tiled=True)
    grad_block = lax.all_gather(grad_out, "row", axis=1, tiled=True)
    log_block = log_all
    dot_block = dot_all
    grad_key, grad_value = run_blocks(
        pair_update,
        (zero_rows, zero_rows),
        (query_block, grad_block, log_block, dot_block),
        block_rows,
    )
    returned = lax.all_to_all(
        jnp.stack([grad_query, grad_key, grad_value])
        .astype(jnp.bfloat16)
        .reshape(3, pairs, rows_dev, width_all, head_dim),
        "col",
        split_axis=3,
        concat_axis=1,
        tiled=True,
    )
    returned = returned.reshape(3, samples, head_count, rows_dev, cols_dev, head_dim)
    projected = jnp.einsum(
        "kshrce,dkhe->srcd",
        returned,
        input_weight.reshape(channels, 3, head_count, head_dim),
        preferred_element_type=jnp.float32,
    )
    return (grad_z.astype(jnp.float32) + projected).astype(jnp.bfloat16)


def solution(mesh):
    in_specs = (
        P(None, "row", "col", None),
        P(None, "row", "col", None),
        P("col", "row", None),
        P("col", "row", None),
        P("col", "row", None),
        P(),
        P(),
        P(),
    )
    out_specs = P(None, "row", "col", None)
    return jax.shard_map(shards, mesh=mesh, in_specs=in_specs, out_specs=out_specs, check_vma=False)
```

profile of v0, /device:TPU:1, one launch (start us, length us, event | category | flops | bytes accessed | tf_op | source)
XLA Modules:
  0.0 482.8 jit_solution(5476060512518797547)
XLA Ops:
  12.8 5.4 %collective-permute-start = (bf16[8,1,6,256]{3,0,2,1:T(8,128)(2,1)S(1)}, bf16[8,1,6,256]{3,0,2,1:T(8,128)(2,1)S(1)}, u32[]{:S(2)}, u32[]{:S(2)}) collective-permute-start(bf16[8,1,6,256]{3,0,2,1:T(8,128)(2,1)S(1)} %get-tuple-element.371), channel_id=1, source_target_pairs={{0,16},{16,32},{32,48},{48,64},{64,80},{80,96},{96,112},{112,128},... | collective-permute-start | bytes 73736 | tf_op jit(solution)/shard_map/ppermute | solution.py:17
  18.1 4.7 collective-permute-start.1
  26.2 4.0 collective-permute-start.3
  34.4 7.8 %all-to-all-start = ((bf16[16,2,1152]{2,1,0:T(2,128)(2,1)}), bf16[16,2,1152]{2,1,0:T(2,128)(2,1)S(1)}, u32[]{:S(2)}, u32[]{:S(2)}) async-start(bf16[16,2,1152]{2,1,0:T(2,128)(2,1)} %reshape.82), calls=%async_computation | async-start | bytes 147456 | tf_op jit(solution)/shard_map/all_to_all | solution.py:83
  42.4 8.3 %all-to-all-done = bf16[16,2,1152]{2,1,0:T(2,128)(2,1)S(1)} async-done(((bf16[16,2,1152]{2,1,0:T(2,128)(2,1)}), bf16[16,2,1152]{2,1,0:T(2,128)(2,1)S(1)}, u32[]{:S(2)}, u32[]{:S(2)}) %all-to-all-start) | async-done | bytes 73760 | tf_op jit(solution)/shard_map/all_to_all | solution.py:83
  51.6 60.1 %all-gather.7.cloned.1.call-done = bf16[2,9216,64]{2,0,1:T(2,128)(2,1)} async-done(((bf16[2,288,64]{2,0,1:T(2,128)(2,1)}), bf16[2,9216,64]{2,0,1:T(2,128)(2,1)}) %all-gather.7.cloned.1.call-update) | async-done | bytes 2359312 | tf_op jit(solution)/shard_map/all_gather | solution.py:105
  111.8 11.1 %copy.104 = bf16[2,8,1152,64]{2,3,0,1:T(8,128)(2,1)} copy(bf16[2,8,1152,64]{3,0,2,1:T(2,128)(2,1)} %bitcast.228) | data formatting | bytes 4718592 | tf_op jit(solution)/shard_map/transpose | solution.py:30
  122.9 83.6 %all-gather.9.cloned.1.call-done = bf16[2,9216,64]{2,0,1:T(2,128)(2,1)} async-done(((bf16[2,288,64]{2,0,1:T(2,128)(2,1)}), bf16[2,9216,64]{2,0,1:T(2,128)(2,1)}) %all-gather.9.cloned.1.call-update) | async-done | bytes 2359312 | tf_op jit(solution)/shard_map/all_gather | solution.py:106
  206.4 11.2 %copy.107 = bf16[2,8,1152,64]{2,3,0,1:T(8,128)(2,1)} copy(bf16[2,8,1152,64]{3,0,2,1:T(2,128)(2,1)} %bitcast.229) | data formatting | bytes 4718592 | tf_op jit(solution)/shard_map/transpose | solution.py:30
  217.6 31.6 %while.39 = (s32[]{:T(128)}, f32[2,288]{1,0:T(2,128)S(1)}, f32[2,288]{1,0:T(2,128)S(1)}, f32[2,288]{1,0:T(2,128)S(1)}, bf16[8,2,1152,64]{2,3,1,0:T(8,128)(2,1)},...) while((s32[]{:T(128)}, f32[2,288]{1,0:T(2,128)S(1)}, ...), condition=%wide.region_4.5_spmd.clone, body=%wide.region_0.4_spmd.clone.sunk | while | flops 174518208 | bytes 8742512 | solution.py:44
  249.3 28.8 %while.40 = (s32[]{:T(128)}, f32[2,288,64]{1,2,0:T(8,128)S(1)}, bf16[8,2,1152,64]{2,3,1,0:T(8,128)(2,1)}, bf16[2,288,64]{1,2,0:T(8,128)(2,1)S(1)}, f32[2,288]{1,...) while((s32[]{:T(128)}, f32[2,288,64]{1,2,0:T(8,128)S(1)}, ...), condition=%wide.region_6.7_spmd.clone, body=%wide.region_5.6_spmd.clone.sunk | while | flops 258232320 | bytes 6641775 | solution.py:44
  250.8 2.0 fusion.166
  254.4 2.0 fusion.166
  265.3 2.0 fusion.166
  272.5 2.0 fusion.166
  276.1 2.0 fusion.166
  278.3 38.2 %all-gather = f32[32,288,2]{1,2,0:T(2,128)S(1)} all-gather(f32[1,288,2]{1,2,0:T(2,128)S(1)} %bitcast.243), channel_id=1, replica_groups=mesh['row'=32,'col'=16] {'row'}, dimensions={0}, use_global_device_ids=true | all-gather | bytes 76032 | tf_op jit(solution)/shard_map/all_gather | solution.py:126
  316.6 37.3 %all-gather.1 = f32[32,288,2]{1,2,0:T(2,128)S(1)} all-gather(f32[1,288,2]{1,2,0:T(2,128)S(1)} %bitcast.242), channel_id=1, replica_groups=mesh['row'=32,'col'=16] {'row'}, dimensions={0}, use_global_device_ids=true | all-gather | bytes 76032 | tf_op jit(solution)/shard_map/all_gather | solution.py:127
  354.1 11.2 %copy.110 = bf16[2,8,1152,64]{2,3,0,1:T(8,128)(2,1)} copy(bf16[2,8,1152,64]{3,0,2,1:T(2,128)(2,1)} %bitcast.226) | data formatting | bytes 4718592 | tf_op jit(solution)/shard_map/transpose | solution.py:30
  365.9 29.7 %all-gather.13.cloned.1.call-done = bf16[2,9216,64]{2,0,1:T(2,128)(2,1)} async-done(((bf16[2,288,64]{2,0,1:T(2,128)(2,1)}), bf16[2,9216,64]{2,0,1:T(2,128)(2,1)}) %all-gather.13.cloned.1.call-update) | async-done | bytes 2359312 | tf_op jit(solution)/shard_map/all_gather | solution.py:152
  395.6 11.1 %copy.112 = bf16[2,8,1152,64]{2,3,0,1:T(8,128)(2,1)} copy(bf16[2,8,1152,64]{3,0,2,1:T(2,128)(2,1)} %bitcast.227) | data formatting | bytes 4718592 | tf_op jit(solution)/shard_map/transpose | solution.py:30
  406.8 48.7 %while.41 = (s32[]{:T(128)}, f32[2,288,64]{1,2,0:T(8,128)S(1)}, f32[2,288,64]{1,2,0:T(8,128)S(1)}, bf16[8,2,1152,64]{2,3,1,0:T(8,128)(2,1)}, bf16[2,288,64]{1,2,...) while((s32[]{:T(128)}, f32[2,288,64]{1,2,0:T(8,128)S(1)}, ...), condition=%wide.region_8.9_spmd.clone, body=%wide.region_7.8_spmd.clone.sunk | while | flops 343904256 | bytes 9973884 | solution.py:44
  457.8 6.6 %all-to-all-start.1 = ((bf16[16,2,3456]{2,1,0:T(2,128)(2,1)}), bf16[16,2,3456]{2,1,0:T(2,128)(2,1)S(1)}, u32[]{:S(2)}, u32[]{:S(2)}) async-start(bf16[16,2,3456]{2,1,0:T(2,128)(2,1)} %reshape.84), calls=%async_computation.1 | async-start | bytes 442368 | tf_op jit(solution)/shard_map/all_to_all | solution.py:161
  464.6 10.1 %all-to-all-done.1 = bf16[16,2,3456]{2,1,0:T(2,128)(2,1)S(1)} async-done(((bf16[16,2,3456]{2,1,0:T(2,128)(2,1)}), bf16[16,2,3456]{2,1,0:T(2,128)(2,1)S(1)}, u32[]{:S(2)}, u32[]{:S(2)}) %all-to-all-start.1) | async-done | bytes 221216 | tf_op jit(solution)/shard_map/all_to_all | solution.py:161
  (195 shorter events, 117.7 us)
Async XLA Ops:
  6.5 26.4 %copy-start = (bf16[256,256]{1,0:T(8,128)(2,1)S(1)}, bf16[256,256]{1,0:T(8,128)(2,1)}, u32[]{:S(2)}) copy-start(bf16[256,256]{1,0:T(8,128)(2,1)} %param.20) | copy-start | bytes 393220
  6.5 24.8 %copy-start.5 = (bf16[8,3,6,256]{3,0,2,1:T(8,128)(2,1)S(1)}, bf16[8,3,6,256]{3,0,2,1:T(8,128)(2,1)}, u32[]{:S(2)}) copy-start(bf16[8,3,6,256]{3,0,2,1:T(8,128)(2,1)} %param.15) | copy-start | bytes 221188
  6.5 24.8 %copy-start.7 = (bf16[3,3,256,256]{3,2,1,0:T(8,128)(2,1)S(1)}, bf16[3,3,256,256]{3,2,1,0:T(8,128)(2,1)}, u32[]{:S(2)}) copy-start(bf16[3,3,256,256]{3,2,1,0:T(8,128)(2,1)} %param.19) | copy-start | bytes 3538948
  6.5 105.2 %all-gather.7.cloned.1.call-start = ((), (), s32[]{:S(2)}) async-start(), calls=%async_computation.2 | async-start | bytes 4866048 | tf_op jit(solution)/shard_map/all_gather | solution.py:105
  8.4 198.0 %all-gather.9.cloned.1.call-start = ((), (), s32[]{:S(2)}) async-start(), calls=%async_computation.3 | async-start | bytes 4866048 | tf_op jit(solution)/shard_map/all_gather | solution.py:106
  10.2 22.5 %copy-start.11 = (bf16[8,3,6,256]{3,0,2,1:T(8,128)(2,1)S(1)}, bf16[8,3,6,256]{3,0,2,1:T(8,128)(2,1)}, u32[]{:S(2)}) copy-start(bf16[8,3,6,256]{3,0,2,1:T(8,128)(2,1)} %param.14) | copy-start | bytes 221188
  10.2 343.9 %all-gather.11.cloned.1.call-start = ((), (), s32[]{:S(2)}) async-start(), calls=%async_computation.4 | async-start | bytes 4866048 | tf_op jit(solution)/shard_map/all_gather | solution.py:151
  12.8 11.2 %collective-permute-start = (bf16[8,1,6,256]{3,0,2,1:T(8,128)(2,1)S(1)}, bf16[8,1,6,256]{3,0,2,1:T(8,128)(2,1)S(1)}, u32[]{:S(2)}, u32[]{:S(2)}) collective-permute-start(bf16[8,1,6,256]{3,0,2,1:T(8,128)(2,1)S(1)} %get-tuple-element.371), channel_id=1, source_target_pairs={{0,16},{16,32},{32,48},{48,64},{64,80},{80,96},{96,112},{112,128},... | collective-permute-start | bytes 73736 | tf_op jit(solution)/shard_map/ppermute | solution.py:17
  18.1 6.8 %collective-permute-start.1 = (bf16[8,1,6,256]{3,0,2,1:T(8,128)(2,1)S(1)}, bf16[8,1,6,256]{3,0,2,1:T(8,128)(2,1)S(1)}, u32[]{:S(2)}, u32[]{:S(2)}) collective-permute-start(bf16[8,1,6,256]{3,0,2,1:T(8,128)(2,1)S(1)} %get-tuple-element.370), channel_id=1, source_target_pairs={{16,0},{32,16},{48,32},{64,48},{80,64},{96,80},{112,96},{128,112},... | collective-permute-start | bytes 73736 | tf_op jit(solution)/shard_map/ppermute | solution.py:19
  24.9 6.7 %collective-permute-start.2 = (bf16[8,5,1,256]{3,0,2,1:T(8,128)(2,1)S(1)}, bf16[8,5,1,256]{3,0,2,1:T(8,128)(2,1)S(1)}, u32[]{:S(2)}, u32[]{:S(2)}) collective-permute-start(bf16[8,5,1,256]{3,0,2,1:T(8,128)(2,1)S(1)} %get-tuple-element.368), channel_id=1, source_target_pairs={{1,0},{2,1},{3,2},{4,3},{5,4},{6,5},{7,6},{8,7},{9,8},{10,9},{11,1... | collective-permute-start | bytes 61448 | tf_op jit(solution)/shard_map/ppermute | solution.py:19
  26.2 5.8 %collective-permute-start.3 = (bf16[8,5,1,256]{3,0,2,1:T(8,128)(2,1)S(1)}, bf16[8,5,1,256]{3,0,2,1:T(8,128)(2,1)S(1)}, u32[]{:S(2)}, u32[]{:S(2)}) collective-permute-start(bf16[8,5,1,256]{3,0,2,1:T(8,128)(2,1)S(1)} %get-tuple-element.369), channel_id=1, source_target_pairs={{0,1},{1,2},{2,3},{3,4},{4,5},{5,6},{6,7},{7,8},{8,9},{9,10},{10,1... | collective-permute-start | bytes 61448 | tf_op jit(solution)/shard_map/ppermute | solution.py:17
  32.9 0.6 copy-start.9
  34.4 16.2 %all-to-all-start = ((bf16[16,2,1152]{2,1,0:T(2,128)(2,1)}), bf16[16,2,1152]{2,1,0:T(2,128)(2,1)S(1)}, u32[]{:S(2)}, u32[]{:S(2)}) async-start(bf16[16,2,1152]{2,1,0:T(2,128)(2,1)} %reshape.82), calls=%async_computation | async-start | bytes 147456 | tf_op jit(solution)/shard_map/all_to_all | solution.py:83
  42.2 353.4 %all-gather.13.cloned.1.call-start = ((), (), s32[]{:S(2)}) async-start(), calls=%async_computation.5 | async-start | bytes 4866048 | tf_op jit(solution)/shard_map/all_gather | solution.py:152
  50.9 0.7 copy-start.6
  206.4 11.2 %copy-start.1 = (bf16[2,288,64]{1,2,0:T(8,128)(2,1)S(1)}, bf16[2,288,64]{1,2,0:T(8,128)(2,1)}, u32[]{:S(2)}) copy-start(bf16[2,288,64]{1,2,0:T(8,128)(2,1)} %param.16) | copy-start | bytes 221188
  395.6 11.2 %copy-start.2 = (f32[2,288,64]{1,2,0:T(8,128)S(1)}, f32[2,288,64]{1,2,0:T(8,128)}, u32[]{:S(2)}) copy-start(f32[2,288,64]{1,2,0:T(8,128)} %custom-call.5) | copy-start | bytes 442372
  395.6 11.2 %copy-start.3 = (bf16[2,288,64]{1,2,0:T(8,128)(2,1)S(1)}, bf16[2,288,64]{1,2,0:T(8,128)(2,1)}, u32[]{:S(2)}) copy-start(bf16[2,288,64]{1,2,0:T(8,128)(2,1)} %param.17) | copy-start | bytes 221188
  395.6 11.2 %copy-start.4 = (bf16[2,288,64]{1,2,0:T(8,128)(2,1)S(1)}, bf16[2,288,64]{1,2,0:T(8,128)(2,1)}, u32[]{:S(2)}) copy-start(bf16[2,288,64]{1,2,0:T(8,128)(2,1)} %param.18) | copy-start | bytes 221188
  455.5 8.9 %copy-start.8 = (bf16[256,768]{1,0:T(8,128)(2,1)S(1)}, bf16[256,768]{1,0:T(8,128)(2,1)}, u32[]{:S(2)}) copy-start(bf16[256,768]{1,0:T(8,128)(2,1)} %param.21) | copy-start | bytes 1179652
  455.8 19.6 %copy-start.10 = (bf16[8,3,6,256]{3,0,2,1:T(8,128)(2,1)S(1)}, bf16[8,3,6,256]{3,0,2,1:T(8,128)(2,1)}, u32[]{:S(2)}) copy-start(bf16[8,3,6,256]{3,0,2,1:T(8,128)(2,1)} %copy-done.9) | copy-start | bytes 221188
  457.8 16.9 %all-to-all-start.1 = ((bf16[16,2,3456]{2,1,0:T(2,128)(2,1)}), bf16[16,2,3456]{2,1,0:T(2,128)(2,1)S(1)}, u32[]{:S(2)}, u32[]{:S(2)}) async-start(bf16[16,2,3456]{2,1,0:T(2,128)(2,1)} %reshape.84), calls=%async_computation.1 | async-start | bytes 442368 | tf_op jit(solution)/shard_map/all_to_all | solution.py:161
Sparse Core Ops, SparseCore 0:
  10.7 101.0 all-gather.6
  115.1 91.2 all-gather.8
  209.8 91.1 all-gather.10
  304.2 91.3 all-gather.12
where the time goes:
time: 486 us; the launch traced here: 483 us
  waiting for transfers between devices  192 us (40%)
  matrix products  101 us (21%)
  blocking collectives  75.5 us (16%)
  local copies, waits for them, and re-layouts  65.1 us (13%)
  starting transfers between devices  29.9 us (6%)
  between operations  13.5 us (3%)
  other arithmetic  4.97 us (1%)
    all_gather x1, waiting for transfers between devices, shards(): lax.all_gather(value_heads, 'row', axis=1, tiled=True)  83.6 us
    all_gather x1, waiting for transfers between devices, shards(): lax.all_gather(key_heads, 'row', axis=1, tiled=True)  60.1 us
    dot_general x32, matrix products, contract(): jnp.einsum('ptd,pud->ptu', left, right, preferred_element_type=jnp.float32)  51.5 us
    transpose x5, local copies, waits for them, and re-layouts, run_blocks(): jnp.moveaxis(member.reshape((member.shape[0], amount // block_rows, block...  45.2 us
    all_gather x1, blocking collectives, shards(): lax.all_gather(log_norm, 'row', axis=1, tiled=True)  38.2 us
    all_gather x1, blocking collectives, shards(): lax.all_gather(row_dot, 'row', axis=1, tiled=True)  37.3 us
    all_gather x1, waiting for transfers between devices, shards(): grad_block = lax.all_gather(grad_out, 'row', axis=1, tiled=True)  29.7 us
    dot_general x8, matrix products, query_update(): jnp.einsum('ptu,pud->ptd', grad_scores, key_block, preferred_element_type...  16.2 us
  transfers between devices with their start and end apart: 10, of which 5 were waited for; matrix products, arithmetic and copies ran while one was open for 22% of the time, Pallas kernels for 0%

commit v1 on v0

v1 whole, which is shorter than its diff:
```python
import functools

import jax
import jax.numpy as jnp
import numpy as np
from jax import lax
from jax.experimental import pallas as pl
from jax.experimental.pallas import tpu as pltpu
from jax.sharding import PartitionSpec as P

BF = jnp.bfloat16
F32 = jnp.float32
SAMPLES, HEADS, HD, C = 8, 4, 64, 256
TR, TC = 3, 6
N_ROW, N_COL = 32, 16
WID = TC * N_COL
STRIP = TR * WID
HALF = STRIP // 2
BLOCK = 8 * STRIP
CHUNK = 256
CHUNKS = BLOCK // CHUNK
PAD = 32
TILE = TR * TC
MESH = pl.DeviceIdType.MESH
FACTOR = HD**-0.5
KAPPA = FACTOR * float(np.log2(np.e))
NT = (((1,), (1,)), ((), ()))


def selections():
    tile = np.zeros((SAMPLES * PAD, TILE * SAMPLES), np.float32)
    for s in range(SAMPLES):
        for t in range(TILE):
            tile[s * PAD + t, t * SAMPLES + s] = 1.0
    strip = np.zeros((STRIP, N_COL * PAD), np.float32)
    for row in range(TR):
        for col in range(WID):
            strip[row * WID + col, (col // TC) * PAD + row * TC + col % TC] = 1.0
    return tile, strip, strip.T


def dot(a, b):
    return jnp.dot(a, b, preferred_element_type=F32)


def dot_nt(a, b):
    return lax.dot_general(a, b, NT, preferred_element_type=F32)


def swap(x):
    return pltpu.roll(x, 64, 1)


def kernel(
    og, zz, qh, kh, vh, cw, ow, iw, sel_tile, sel_strip, sel_back,
    out,
    xp, gz_keep, ga_s, do_r, qpk, opk, kvpk, q_r, o_r, kv_r, qz, oz, do_t, k_t, v_t1,
    o_t, st_s, st_r, kvo, kv_part, dq_t, qo, q_part, g_s, g_r,
    halo_send, halo_recv, a_send, a_recv, q_send, q_recv, o_send, o_recv,
    k_send, k_recv, t_send, t_recv, p_send, p_recv, d_send, d_recv, b_send, b_recv,
):
    r = lax.axis_index("row")
    c = lax.axis_index("col")
    core = lax.rem(r, 2)
    other = 1 - core
    zi = lax.rem(r // 2, 8)
    xh = r // 16
    zl = lax.rem(zi, 2)
    nq = xh * 2 + zl
    nk = zi // 2

    def q_base(n):
        return (n // 2) * 16 + (2 * nk + lax.rem(n, 2)) * 2

    def k_base(n):
        return xh * 16 + (2 * n + zl) * 2

    def wrap(x, n):
        return lax.rem(x + n, n)

    lanes = lax.broadcasted_iota(jnp.int32, (HALF, 128), 1) < 64
    lanes_strip = lax.broadcasted_iota(jnp.int32, (STRIP, 128), 1) < 64
    lanes_chunk = lax.broadcasted_iota(jnp.int32, (CHUNK, 128), 1) < 64

    barrier = pltpu.get_barrier_semaphore()
    shifts = [(i, j) for i in (-1, 0, 1) for j in (-1, 0, 1) if (i, j) != (0, 0)]
    peers = [(wrap(r + i, N_ROW), wrap(c + j, N_COL)) for i, j in shifts]
    peers += [(r, lax.rem(c + o, N_COL)) for o in range(2, N_COL - 1)]
    for base, own in ((q_base, nq), (k_base, nk)):
        for o in range(1, 4):
            n = lax.rem(own + o, 4)
            peers += [(base(n), c), (base(n) + 1, c)]
    peers += [(r + 1 - 2 * core, c)]
    for peer in peers:
        pl.semaphore_signal(barrier, inc=1, device_id=peer, device_id_type=MESH)

    for p in range(2):
        qpk[p] = jnp.concatenate([qh[p, :HALF, :], qh[p, HALF:, :]], axis=1)
        kvpk[p] = jnp.concatenate([kh[p], vh[p]], axis=1)
    xp[1:4, 1:7] = og[...]
    pl.semaphore_wait(barrier, len(peers))

    def push(src, dst, send, recv, peer):
        copy = pltpu.make_async_remote_copy(
            src_ref=src, dst_ref=dst, send_sem=send, recv_sem=recv,
            device_id=peer, device_id_type=MESH,
        )
        return copy

    def rim(shift, width, take):
        if shift == 0:
            return pl.ds(0, width) if take else pl.ds(1, width)
        if take:
            return pl.ds(width - 1, 1) if shift == 1 else pl.ds(0, 1)
        return pl.ds(0, 1) if shift == 1 else pl.ds(width + 1, 1)

    halos = []
    for index, (i, j) in enumerate(shifts):
        halos.append(
            push(
                og.at[rim(i, TR, True), rim(j, TC, True)],
                xp.at[rim(i, TR, False), rim(j, TC, False)],
                halo_send.at[index], halo_recv.at[index],
                (wrap(r + i, N_ROW), wrap(c + j, N_COL)),
            )
        )
    for copy in halos:
        copy.start()

    def gather(src, dst, base, own, send, recv):
        slot = own * 2 + core
        started, arrivals = [], []
        dst[slot] = src[core]
        started.append(
            push(src.at[other], dst.at[slot], send.at[0], recv.at[0], (r + 1 - 2 * core, c))
        )
        arrivals.append(
            push(src.at[0], dst.at[own * 2 + other], send.at[0], recv.at[0],
                 (r + 1 - 2 * core, c))
        )
        for o in range(1, 4):
            n = lax.rem(own + o, 4)
            back = lax.rem(own + 4 - o, 4)
            for p in range(2):
                place = 1 + (o - 1) * 2
                started.append(
                    push(src.at[p], dst.at[slot], send.at[place + p], recv.at[place + core],
                         (base(n) + p, c))
                )
                arrivals.append(
                    push(src.at[p], dst.at[back * 2 + p], send.at[place + p],
                         recv.at[place + p], (base(back) + p, c))
                )
        for copy in started:
            copy.start()
        return started, arrivals

    kv_out, kv_in = gather(kvpk, kv_r, k_base, nk, k_send, k_recv)
    q_out, q_in = gather(qpk, q_r, q_base, nq, q_send, q_recv)

    for copy in halos:
        copy.wait_recv()
    zero_row = jnp.zeros((1, TC + 2, SAMPLES, C), BF)
    zero_col = jnp.zeros((TR + 2, 1, SAMPLES, C), BF)

    @pl.when(r == 0)
    def _():
        xp[0:1] = zero_row

    @pl.when(r == N_ROW - 1)
    def _():
        xp[TR + 1 : TR + 2] = zero_row

    @pl.when(c == 0)
    def _():
        xp[:, 0:1] = zero_col

    @pl.when(c == N_COL - 1)
    def _():
        xp[:, TC + 1 : TC + 2] = zero_col

    cells = xp[...].astype(F32)
    conv = jnp.zeros((TILE * SAMPLES, C), F32)
    for a in (-1, 0, 1):
        for b in (-1, 0, 1):
            window = cells[1 - a : 1 - a + TR, 1 - b : 1 - b + TC]
            window = window.reshape(TILE * SAMPLES, C).astype(BF)
            conv = conv + dot_nt(window, cw[a + 1, b + 1])
    z = zz[...].astype(F32).reshape(TILE * SAMPLES, C)
    sig = jax.nn.sigmoid(z)
    grad_z = (conv * sig * (1.0 + z * (1.0 - sig))).astype(BF)
    placed = dot(sel_tile[...], grad_z)
    gz_keep[...] = placed
    ga = dot_nt(placed.astype(BF), ow[...]).astype(BF)
    for s in range(SAMPLES):
        for b in range(2):
            ga_s[2 * s + b] = ga[s * PAD : (s + 1) * PAD, b * 128 : (b + 1) * 128]

    def exchange(src, dst, send, recv):
        dst[c] = src[c]
        started, arrivals = [], []
        for o in range(1, N_COL):
            to, back = lax.rem(c + o, N_COL), lax.rem(c + N_COL - o, N_COL)
            started.append(push(src.at[to], dst.at[c], send.at[o], recv.at[o], (r, to)))
            arrivals.append(push(src.at[back], dst.at[back], send.at[o], recv.at[o], (r, back)))
        for copy in started:
            copy.start()
        return started, arrivals

    a_out, a_in = exchange(ga_s, do_r, a_send, a_recv)
    for copy in a_in:
        copy.wait_recv()
    strip = dot(sel_strip[...], do_r[...].reshape(N_COL * PAD, 128))
    top, bottom = strip[:HALF], strip[HALF:]
    opk[0] = jnp.where(lanes, top, swap(bottom)).astype(BF)
    opk[1] = jnp.where(lanes, swap(top), bottom).astype(BF)
    o_out, o_in = gather(opk, o_r, q_base, nq, o_send, o_recv)

    for copy in q_in + kv_in:
        copy.wait_recv()
    for k in range(8):
        x = q_r[k].astype(F32)
        qz[k * STRIP : k * STRIP + HALF] = jnp.where(lanes, x, 0.0).astype(BF)
        qz[k * STRIP + HALF : (k + 1) * STRIP] = jnp.where(lanes, swap(x), 0.0).astype(BF)
    keys = kv_r.reshape(BLOCK, 128)
    v_t1[:, 64:80, :] = jnp.ones((CHUNKS, 16, CHUNK), BF)
    for k in range(CHUNKS):
        turned = keys[k * CHUNK : (k + 1) * CHUNK].astype(F32).T.astype(BF)
        k_t[k] = turned[:64]
        v_t1[k, 0:64, :] = turned[64:]

    def stats_step(j, carry):
        at = pl.multiple_of(j * CHUNK, CHUNK)
        scores = dot_nt(keys[...], qz[pl.ds(at, CHUNK)])
        top = jnp.max(scores, axis=0, keepdims=True) * KAPPA
        e = jnp.exp2(scores * KAPPA - top)
        st_s[0:1, pl.ds(at, CHUNK)] = top
        st_s[1:2, pl.ds(at, CHUNK)] = jnp.sum(e, axis=0, keepdims=True)
        eb = e.astype(BF)
        acc = jnp.zeros((80, CHUNK), F32)
        for k in range(CHUNKS):
            acc = acc + dot(v_t1[k], eb[k * CHUNK : (k + 1) * CHUNK])
        st_s[2:3, pl.ds(at, CHUNK)] = acc[64:65]
        o_t[:, pl.ds(at, CHUNK)] = acc[:64]
        return carry

    lax.fori_loop(0, CHUNKS, stats_step, 0)

    for copy in o_in:
        copy.wait_recv()
    for k in range(8):
        x = o_r[k].astype(F32)
        oz[k * STRIP : k * STRIP + HALF] = jnp.where(lanes, 0.0, swap(x)).astype(BF)
        oz[k * STRIP + HALF : (k + 1) * STRIP] = jnp.where(lanes, 0.0, x).astype(BF)
    for k in range(CHUNKS):
        at = slice(k * CHUNK, (k + 1) * CHUNK)
        do_t[:, at] = oz[at].astype(F32).T[64:]
    st_s[3:4] = jnp.sum(o_t[...] * do_t[...], axis=0, keepdims=True)

    st_r[nq] = st_s[...]
    t_out, t_in = [], []
    for o in range(1, 4):
        n, back = lax.rem(nq + o, 4), lax.rem(nq + 4 - o, 4)
        t_out.append(push(st_s, st_r.at[nq], t_send.at[o], t_recv.at[o], (q_base(n) + core, c)))
        t_in.append(
            push(st_s, st_r.at[back], t_send.at[o], t_recv.at[o], (q_base(back) + core, c))
        )
    for copy in t_out:
        copy.start()
    for copy in t_in:
        copy.wait_recv()
    tops = [st_r[n, 0:1] for n in range(4)]
    top = jnp.maximum(jnp.maximum(tops[0], tops[1]), jnp.maximum(tops[2], tops[3]))
    norm = norm_b = weighted = jnp.zeros((1, BLOCK), F32)
    for n in range(4):
        scale = jnp.exp2(tops[n] - top)
        norm = norm + scale * st_r[n, 1:2]
        norm_b = norm_b + scale * st_r[n, 2:3]
        weighted = weighted + scale * st_r[n, 3:4]
    log_norm = top + jnp.log(norm) * float(np.log2(np.e))
    row_dot = weighted / norm_b

    dq_t[...] = jnp.zeros_like(dq_t)
    mine = nk * 2 + core

    def part_copy(k):
        at = pl.multiple_of(k * STRIP, 32)
        return push(
            kvo.at[pl.ds(at, STRIP)], kv_part.at[core, nk], p_send.at[k],
            p_recv.at[core, nk], (k_base(k // 2) + lax.rem(k, 2), c),
        )

    def grad_step(j, carry):
        at = pl.multiple_of(j * CHUNK, CHUNK)
        kv = keys[pl.ds(at, CHUNK)]
        probs = jnp.exp2(dot_nt(kv, qz[...]) * KAPPA - log_norm)
        grad_probs = dot_nt(kv, oz[...])
        grad_scores = (probs * (grad_probs - row_dot)).astype(BF)
        both = dot(grad_scores, qz[...]) + dot(probs.astype(BF), oz[...])
        kvo[pl.ds(at, CHUNK)] = jnp.where(lanes_chunk, both * FACTOR, both).astype(BF)
        dq_t[0:64] += dot(k_t[j], grad_scores)
        k = j - 1

        @pl.when(jnp.logical_and(k >= 0, k != mine))
        def _():
            part_copy(k).start()

        return carry

    lax.fori_loop(0, CHUNKS, grad_step, 0)
    kv_part[core, nk] = kvo[pl.ds(pl.multiple_of(mine * STRIP, 32), STRIP)]

    turned = dq_t[...].T * FACTOR
    for k in range(8):
        first = turned[k * STRIP : k * STRIP + HALF]
        second = turned[k * STRIP + HALF : (k + 1) * STRIP]
        qo[k] = (first + swap(second)).astype(BF)
    mine_q = nq * 2 + core
    q_part[core, nq] = qo[mine_q]

    def dq_copy(k):
        return push(
            qo.at[k], q_part.at[core, nq], d_send.at[k], d_recv.at[core, nq],
            (q_base(k // 2) + k % 2, c),
        )

    for k in range(8):

        @pl.when(k != mine_q)
        def _():
            dq_copy(k).start()

    def arrive(dst, recv, base, own, src):
        for p in range(2):
            for n in range(4):

                @pl.when(jnp.logical_or(n != own, p != core))
                def _():
                    push(src, dst.at[p, n], d_send.at[0], recv.at[p, n],
                         (base(n) + p, c)).wait_recv()

    arrive(kv_part, p_recv, k_base, nk, kvo.at[pl.ds(0, STRIP)])
    arrive(q_part, d_recv, q_base, nq, qo.at[0])
    kv0, kv1 = [
        kv_part[p, 0].astype(F32) + kv_part[p, 1].astype(F32)
        + kv_part[p, 2].astype(F32) + kv_part[p, 3].astype(F32)
        for p in range(2)
    ]
    q0, q1 = [
        q_part[p, 0].astype(F32) + q_part[p, 1].astype(F32)
        + q_part[p, 2].astype(F32) + q_part[p, 3].astype(F32)
        for p in range(2)
    ]
    dq_top = jnp.where(lanes, q0, swap(q1))
    dq_bottom = jnp.where(lanes, swap(q0), q1)
    dk = jnp.where(lanes_strip, kv0, swap(kv1)).astype(BF)
    dv = jnp.where(lanes_strip, swap(kv0), kv1).astype(BF)
    back = sel_back[...]
    placed_q = (
        dot(back[:, :HALF], dq_top.astype(BF)) + dot(back[:, HALF:], dq_bottom.astype(BF))
    )
    for kind, placed in enumerate((placed_q, dot(back, dk), dot(back, dv))):
        placed = placed.astype(BF)
        for n in range(N_COL):
            g_s[n, :, kind * 128 : (kind + 1) * 128] = placed[n * PAD : (n + 1) * PAD]
    b_out, b_in = exchange(g_s, g_r, b_send, b_recv)
    for copy in b_in:
        copy.wait_recv()

    total = gz_keep[...]
    for b in range(2):
        got = jnp.concatenate([g_r[2 * s + b] for s in range(SAMPLES)], axis=0)
        for kind in range(3):
            weight = iw[:, kind * 256 + b * 128 : kind * 256 + (b + 1) * 128]
            total = total + dot_nt(got[:, kind * 128 : (kind + 1) * 128], weight)
    out[...] = total.astype(BF)

    for copy in halos + kv_out + q_out + a_out + o_out + t_out + b_out:
        copy.wait_send()
    for k in range(8):

        @pl.when(k != mine)
        def _():
            part_copy(k).wait_send()

        @pl.when(k != mine_q)
        def _():
            dq_copy(k).wait_send()


def shards(
    pre_silu, out_grad, query_heads, key_heads, value_heads, conv_weight, out_weight, input_weight
):
    sel_tile, sel_strip, sel_back = [jnp.asarray(x, BF) for x in selections()]
    og = jnp.transpose(out_grad, (1, 2, 0, 3))
    zz = jnp.transpose(pre_silu, (1, 2, 0, 3))
    vmem = pl.BlockSpec(memory_space=pltpu.VMEM)
    dma = lambda *n: pltpu.SemaphoreType.DMA(n)
    result = pl.pallas_call(
        kernel,
        out_shape=jax.ShapeDtypeStruct((SAMPLES * PAD, C), BF),
        in_specs=[vmem] * 11,
        out_specs=vmem,
        scratch_shapes=[
            pltpu.VMEM((TR + 2, TC + 2, SAMPLES, C), BF),
            pltpu.VMEM((SAMPLES * PAD, C), F32),
            pltpu.VMEM((N_COL, PAD, 128), BF),
            pltpu.VMEM((N_COL, PAD, 128), BF),
            pltpu.VMEM((2, HALF, 128), BF),
            pltpu.VMEM((2, HALF, 128), BF),
            pltpu.VMEM((2, STRIP, 128), BF),
            pltpu.VMEM((8, HALF, 128), BF),
            pltpu.VMEM((8, HALF, 128), BF),
            pltpu.VMEM((8, STRIP, 128), BF),
            pltpu.VMEM((BLOCK, 128), BF),
            pltpu.VMEM((BLOCK, 128), BF),
            pltpu.VMEM((64, BLOCK), F32),
            pltpu.VMEM((CHUNKS, 64, CHUNK), BF),
            pltpu.VMEM((CHUNKS, 80, CHUNK), BF),
            pltpu.VMEM((64, BLOCK), F32),
            pltpu.VMEM((4, BLOCK), F32),
            pltpu.VMEM((4, 4, BLOCK), F32),
            pltpu.VMEM((BLOCK, 128), BF),
            pltpu.VMEM((2, 4, STRIP, 128), BF),
            pltpu.VMEM((128, BLOCK), F32),
            pltpu.VMEM((8, HALF, 128), BF),
            pltpu.VMEM((2, 4, HALF, 128), BF),
            pltpu.VMEM((N_COL, PAD, 384), BF),
            pltpu.VMEM((N_COL, PAD, 384), BF),
            dma(8), dma(8), dma(16), dma(16), dma(7), dma(7), dma(7), dma(7),
            dma(7), dma(7), dma(4), dma(4), dma(8), dma(2, 4), dma(8), dma(2, 4),
            dma(16), dma(16),
        ],
        compiler_params=pltpu.CompilerParams(
            collective_id=0, has_side_effects=True, vmem_limit_bytes=56 * 2**20
        ),
    )(
        og, zz, query_heads, key_heads, value_heads, conv_weight, out_weight, input_weight,
        sel_tile, sel_strip, sel_back,
    )
    result = result.reshape(SAMPLES, PAD, C)[:, :TILE]
    return result.reshape(SAMPLES, TR, TC, C)


def solution(mesh):
    in_specs = (
        P(None, "row", "col", None),
        P(None, "row", "col", None),
        P("col", "row", None),
        P("col", "row", None),
        P("col", "row", None),
        P(),
        P(),
        P(),
    )
    out_specs = P(None, "row", "col", None)
    return jax.shard_map(shards, mesh=mesh, in_specs=in_specs, out_specs=out_specs, check_vma=False)
```

time: 486 us -> 103 us (0.21)
  the two profiles are of different devices: /device:TPU:1 before, /device:TPU:4 now
where the time goes in v1:
time: 103 us; the launch traced here: 102 us
  Pallas kernels  95.7 us (93%)
  local copies, waits for them, and re-layouts  6.61 us (6%)
    pallas_call x1, Pallas kernels, shards(): pl.pallas_call(kernel, out_shape=jax.ShapeDtypeStruct((SAMPLES * PAD, C),...  95.7 us
    unnamed x3, local copies, waits for them, and re-layouts  5.06 us

profile of v1, /device:TPU:4, one launch (start us, length us, event | category | flops | bytes accessed | tf_op | source)
XLA Modules:
  0.0 102.3 jit_solution(16295242395405635581)
XLA Ops:
  0.0 1.7 %copy.12.qh = bf16[2,288,64]{2,1,0:T(8,128)(2,1)} copy(bf16[2,288,64]{1,2,0:T(8,128)(2,1)} %param.13) | data formatting | bytes 147456 | tf_op args[2]
  1.7 1.7 %copy.13.kh = bf16[2,288,64]{2,1,0:T(8,128)(2,1)} copy(bf16[2,288,64]{1,2,0:T(8,128)(2,1)} %param.14) | data formatting | bytes 147456 | tf_op args[3]
  3.4 1.7 %copy.14.vh = bf16[2,288,64]{2,1,0:T(8,128)(2,1)} copy(bf16[2,288,64]{1,2,0:T(8,128)(2,1)} %param.15) | data formatting | bytes 147456 | tf_op args[4]
  5.1 95.7 %shard_map.109 = bf16[256,256]{1,0:T(8,128)(2,1)} custom-call(bf16[3,6,8,256]{3,2,1,0:T(8,128)(2,1)} %bitcast.5, bf16[3,6,8,256]{3,2,1,0:T(8,128)(2,1)} %bitcast.6, bf16[2,288,64]{2,1,0:T(8,128)(2,1)} %copy.12.qh, bf16[2,288,64]{2,1,0:T(8,128)(2,1)} %copy.13.kh, bf16[2,288,64]{2,1,0:T(8,128)(2,1)} %copy.14.vh, bf16[3,3,256,256]{3,2,1,0:T(8,128)(2,1)} %cw.1, ...), custom_call_target="tpu_custom_call" | custom-call | tf_op jit(solution)/shard_map/pallas_call | solution.py:399
  100.7 0.9 slice.4
  101.6 0.6 copy.15

commit v2 on v1

v2 whole, which is shorter than its diff:
```python
import functools

import jax
import jax.numpy as jnp
import numpy as np
from jax import lax
from jax.experimental import pallas as pl
from jax.experimental.pallas import tpu as pltpu
from jax.sharding import PartitionSpec as P

BF = jnp.bfloat16
F32 = jnp.float32
SAMPLES, HEADS, HD, C = 8, 4, 64, 256
TR, TC = 3, 6
N_ROW, N_COL = 32, 16
WID = TC * N_COL
STRIP = TR * WID
HALF = STRIP // 2
BLOCK = 8 * STRIP
CHUNK = 256
CHUNKS = BLOCK // CHUNK
PAD = 32
TILE = TR * TC
MESH = pl.DeviceIdType.MESH
FACTOR = HD**-0.5
KAPPA = FACTOR * float(np.log2(np.e))
NT = (((1,), (1,)), ((), ()))


REST = STRIP - CHUNK
MSG = 48


def spot(half, token):
    return half * 16 + token if token < 16 else 32 + half * 2 + token - 16


def selections():
    tile = np.zeros((SAMPLES * PAD, TILE * SAMPLES), np.float32)
    strip = np.zeros((STRIP, N_COL * PAD), np.float32)
    back = np.zeros((N_COL * MSG, 2 * STRIP), np.float32)
    got = np.zeros((2 * TILE * SAMPLES, N_COL * MSG), np.float32)
    for t in range(TILE):
        for s in range(SAMPLES):
            tile[s * PAD + t, t * SAMPLES + s] = 1.0
        for n in range(N_COL):
            place = (t // TC) * WID + n * TC + t % TC
            strip[place, n * PAD + t] = 1.0
            for half in range(2):
                back[n * MSG + spot(half, t), half * STRIP + place] = 1.0
                row = half * TILE * SAMPLES + t * SAMPLES + n // 2
                got[row, n * MSG + spot(half, t)] = 1.0
    return tile, strip, back, got


def dot(a, b):
    return jnp.dot(a, b, preferred_element_type=F32)


def dot_nt(a, b):
    return lax.dot_general(a, b, NT, preferred_element_type=F32)


def swap(x):
    return pltpu.roll(x, 64, 1)


def kernel(
    og, zz, qh, kh, vh, cw, ow, iw, sel_tile, sel_strip, sel_back, sel_got,
    out,
    xp, gz_keep, ga_s, do_r, qpk, opk, kvpk, q_r, o_r, kv_r, qz, oz, do_t, k_t, v_t1,
    o_t, st_s, st_r, kvo, kv_part, dq_t, qo, q_part, g_s, g_r,
    halo_send, halo_recv, a_send, a_recv, q_send, q_recv, o_send, o_recv,
    k_send, k_recv, t_send, t_recv, p_send, p_recv, d_send, d_recv, b_send, b_recv,
):
    r = lax.axis_index("row")
    c = lax.axis_index("col")
    core = lax.rem(r, 2)
    other = 1 - core
    zi = lax.rem(r // 2, 8)
    xh = r // 16
    zl = lax.rem(zi, 2)
    mq = zi // 2

    def q_peer(o):
        return xh * 16 + (2 * lax.rem(mq + o, 4) + zl) * 2

    def k_peer(o):
        return lax.rem(xh + o // 2, 2) * 16 + (2 * mq + lax.rem(zl + lax.rem(o, 2), 2)) * 2

    def wrap(x, n):
        return lax.rem(x + n, n)

    lanes = lax.broadcasted_iota(jnp.int32, (HALF, 128), 1) < 64
    lanes_strip = lax.broadcasted_iota(jnp.int32, (STRIP, 128), 1) < 64
    lanes_chunk = lax.broadcasted_iota(jnp.int32, (CHUNK, 128), 1) < 64

    barrier = pltpu.get_barrier_semaphore()
    shifts = [(i, j) for i in (-1, 0, 1) for j in (-1, 0, 1) if (i, j) != (0, 0)]
    peers = [(wrap(r + i, N_ROW), wrap(c + j, N_COL)) for i, j in shifts]
    peers += [(r, lax.rem(c + o, N_COL)) for o in range(2, N_COL - 1)]
    for peer in (q_peer, k_peer):
        for o in range(1, 4):
            peers += [(peer(o), c), (peer(o) + 1, c)]
    peers += [(r + 1 - 2 * core, c)]
    for peer in peers:
        pl.semaphore_signal(barrier, inc=1, device_id=peer, device_id_type=MESH)

    def halves(x, dst):
        top, bottom = x[:HALF], x[HALF:]
        dst[0] = jnp.where(lanes, top, swap(bottom)).astype(BF)
        dst[1] = jnp.where(lanes, swap(top), bottom).astype(BF)

    for p in range(2):
        kvpk[p] = jnp.concatenate([kh[p], vh[p]], axis=0).T
    halves(jnp.concatenate([qh[0], qh[1]], axis=0).T.astype(F32), qpk)
    xp[1:4, 1:7] = og[...]
    pl.semaphore_wait(barrier, len(peers))

    def push(src, dst, send, recv, peer):
        copy = pltpu.make_async_remote_copy(
            src_ref=src, dst_ref=dst, send_sem=send, recv_sem=recv,
            device_id=peer, device_id_type=MESH,
        )
        return copy

    def rim(shift, width, take):
        if shift == 0:
            return pl.ds(0, width) if take else pl.ds(1, width)
        if take:
            return pl.ds(width - 1, 1) if shift == 1 else pl.ds(0, 1)
        return pl.ds(0, 1) if shift == 1 else pl.ds(width + 1, 1)

    halos = []
    for index, (i, j) in enumerate(shifts):
        halos.append(
            push(
                og.at[rim(i, TR, True), rim(j, TC, True)],
                xp.at[rim(i, TR, False), rim(j, TC, False)],
                halo_send.at[index], halo_recv.at[index],
                (wrap(r + i, N_ROW), wrap(c + j, N_COL)),
            )
        )
    for copy in halos:
        copy.start()

    def gather(src, dst, peer, slot, turn, order, send, recv):
        here = (r + 1 - 2 * core, c)
        dst[slot(0) * 2 + core] = src[core]
        started = [
            push(src.at[other], dst.at[slot(0) * 2 + core], send.at[0], recv.at[0], here)
        ]
        arrivals = {
            0: [push(src.at[0], dst.at[slot(0) * 2 + other], send.at[0], recv.at[0], here)]
        }
        for o in order:
            there = turn(o)
            arrivals[o] = []
            for p in range(2):
                started.append(
                    push(src.at[p], dst.at[slot(o, True) * 2 + core], send.at[2 * o + p],
                         recv.at[2 * there + core], (peer(o) + p, c))
                )
                arrivals[o].append(
                    push(src.at[p], dst.at[slot(o) * 2 + p], send.at[2 * o + p],
                         recv.at[2 * o + p], (peer(o) + p, c))
                )
        for copy in started:
            copy.start()
        return started, arrivals

    def k_slot(o, remote=False):
        return 3 - o

    def q_slot(o, remote=False):
        return mq if remote else lax.rem(mq + o, 4)

    ring = lambda o: (4 - o) % 4
    kv_out, kv_in = gather(kvpk, kv_r, k_peer, k_slot, lambda o: o, (1, 2, 3), k_send, k_recv)
    q_out, q_in = gather(qpk, q_r, q_peer, q_slot, ring, (1, 3, 2), q_send, q_recv)

    for copy in halos:
        copy.wait_recv()
    zero_row = jnp.zeros((1, TC + 2, SAMPLES, C), BF)
    zero_col = jnp.zeros((TR + 2, 1, SAMPLES, C), BF)

    @pl.when(r == 0)
    def _():
        xp[0:1] = zero_row

    @pl.when(r == N_ROW - 1)
    def _():
        xp[TR + 1 : TR + 2] = zero_row

    @pl.when(c == 0)
    def _():
        xp[:, 0:1] = zero_col

    @pl.when(c == N_COL - 1)
    def _():
        xp[:, TC + 1 : TC + 2] = zero_col

    cells = xp[...].astype(F32)
    conv = jnp.zeros((TILE * SAMPLES, C), F32)
    for a in (-1, 0, 1):
        for b in (-1, 0, 1):
            window = cells[1 - a : 1 - a + TR, 1 - b : 1 - b + TC]
            window = window.reshape(TILE * SAMPLES, C).astype(BF)
            conv = conv + dot_nt(window, cw[a + 1, b + 1])
    z = zz[...].astype(F32).reshape(TILE * SAMPLES, C)
    sig = jax.nn.sigmoid(z)
    grad_z = (conv * sig * (1.0 + z * (1.0 - sig))).astype(BF)
    gz_keep[...] = grad_z.astype(F32)
    placed = dot(sel_tile[...], grad_z)
    ga = dot_nt(placed.astype(BF), ow[...]).astype(BF)
    for s in range(SAMPLES):
        for b in range(2):
            ga_s[2 * s + b] = ga[s * PAD : (s + 1) * PAD, b * 128 : (b + 1) * 128]

    def exchange(src, dst, send, recv):
        dst[c] = src[c]
        started, arrivals = [], []
        for o in range(1, N_COL):
            to, back = lax.rem(c + o, N_COL), lax.rem(c + N_COL - o, N_COL)
            started.append(push(src.at[to], dst.at[c], send.at[o], recv.at[o], (r, to)))
            arrivals.append(
                push(src.at[back], dst.at[back], send.at[o], recv.at[o], (r, back))
            )
        for copy in started:
            copy.start()
        return started, arrivals

    a_out, a_in = exchange(ga_s, do_r, a_send, a_recv)

    def unpack(src, slot, dst, left):
        x = src[slot].astype(F32)
        if left:
            top, bottom = jnp.where(lanes, x, 0.0), jnp.where(lanes, swap(x), 0.0)
        else:
            top, bottom = jnp.where(lanes, 0.0, swap(x)), jnp.where(lanes, 0.0, x)
        bottom = bottom.astype(BF)
        at = pl.multiple_of(slot * CHUNK, CHUNK)
        dst[pl.ds(at, HALF)] = top.astype(BF)
        dst[pl.ds(at + HALF, CHUNK - HALF)] = bottom[: CHUNK - HALF]
        rest = pl.multiple_of(8 * CHUNK + slot * REST, REST)
        dst[pl.ds(rest, REST)] = bottom[CHUNK - HALF :]

    for o in range(4):
        for copy in kv_in[o]:
            copy.wait_recv()
    keys = kv_r.reshape(BLOCK, 128)
    v_t1[:, 64:80, :] = jnp.ones((CHUNKS, 16, CHUNK), BF)
    for k in range(CHUNKS):
        turned = keys[k * CHUNK : (k + 1) * CHUNK].astype(F32).T.astype(BF)
        k_t[k] = turned[:64]
        v_t1[k, 0:64, :] = turned[64:]

    def stats_chunk(at):
        scores = dot_nt(keys[...], qz[pl.ds(at, CHUNK)])
        top = jnp.max(scores, axis=0, keepdims=True) * KAPPA
        e = jnp.exp2(scores * KAPPA - top)
        st_s[0:1, pl.ds(at, CHUNK)] = top
        st_s[1:2, pl.ds(at, CHUNK)] = jnp.sum(e, axis=0, keepdims=True)
        eb = e.astype(BF)
        acc = jnp.zeros((80, CHUNK), F32)
        for k in range(CHUNKS):
            acc = acc + dot(v_t1[k], eb[k * CHUNK : (k + 1) * CHUNK])
        st_s[2:3, pl.ds(at, CHUNK)] = acc[64:65]
        o_t[:, pl.ds(at, CHUNK)] = acc[:64]

    def stats_member(o):
        for copy in q_in[o]:
            copy.wait_recv()

        def step(k, carry):
            slot = q_slot(o) * 2 + k
            unpack(q_r, slot, qz, True)
            stats_chunk(pl.multiple_of(slot * CHUNK, CHUNK))
            return carry

        lax.fori_loop(0, 2, step, 0)

    stats_member(0)
    for copy in a_in:
        copy.wait_recv()
    halves(dot(sel_strip[...], do_r[...].reshape(N_COL * PAD, 128)), opk)
    o_out, o_in = gather(opk, o_r, q_peer, q_slot, ring, (1, 3, 2), o_send, o_recv)
    for o in (1, 3, 2):
        stats_member(o)
    stats_chunk(8 * CHUNK)

    for o in range(4):
        for copy in o_in[o]:
            copy.wait_recv()
    for k in range(8):
        unpack(o_r, k, oz, False)
    for k in range(CHUNKS):
        at = slice(k * CHUNK, (k + 1) * CHUNK)
        do_t[:, at] = oz[at].astype(F32).T[64:]
    st_s[3:4] = jnp.sum(o_t[...] * do_t[...], axis=0, keepdims=True)

    st_r[0] = st_s[...]
    t_out, t_in = [], []
    for o in range(1, 4):
        peer = (q_peer(o) + core, c)
        t_out.append(push(st_s, st_r.at[ring(o)], t_send.at[o], t_recv.at[ring(o)], peer))
        t_in.append(push(st_s, st_r.at[o], t_send.at[o], t_recv.at[o], peer))
    for copy in t_out:
        copy.start()
    for copy in t_in:
        copy.wait_recv()
    tops = [st_r[n, 0:1] for n in range(4)]
    top = jnp.maximum(jnp.maximum(tops[0], tops[1]), jnp.maximum(tops[2], tops[3]))
    norm = norm_b = weighted = jnp.zeros((1, BLOCK), F32)
    for n in range(4):
        scale = jnp.exp2(tops[n] - top)
        norm = norm + scale * st_r[n, 1:2]
        norm_b = norm_b + scale * st_r[n, 2:3]
        weighted = weighted + scale * st_r[n, 3:4]
    log_norm = top + jnp.log(norm) * float(np.log2(np.e))
    row_dot = weighted / norm_b

    dq_t[...] = jnp.zeros_like(dq_t)
    mine = 6 + core

    def part_copy(k):
        at = pl.multiple_of(k * STRIP, 32)
        o = 3 - k // 2
        return push(
            kvo.at[pl.ds(at, STRIP)], kv_part.at[core, o], p_send.at[k],
            p_recv.at[core, o], (k_peer(o) + lax.rem(k, 2), c),
        )

    def grad_step(j, carry):
        at = pl.multiple_of(j * CHUNK, CHUNK)
        kv = keys[pl.ds(at, CHUNK)]
        probs = jnp.exp2(dot_nt(kv, qz[...]) * KAPPA - log_norm)
        grad_probs = dot_nt(kv, oz[...])
        grad_scores = (probs * (grad_probs - row_dot)).astype(BF)
        both = dot(grad_scores, qz[...]) + dot(probs.astype(BF), oz[...])
        kvo[pl.ds(at, CHUNK)] = jnp.where(lanes_chunk, both * FACTOR, both).astype(BF)
        dq_t[0:64] += dot(k_t[j], grad_scores)
        k = j - 1

        @pl.when(jnp.logical_and(k >= 0, k != mine))
        def _():
            part_copy(k).start()

        return carry

    lax.fori_loop(0, CHUNKS, grad_step, 0)
    kv_part[core, 0] = kvo[pl.ds(pl.multiple_of(mine * STRIP, 32), STRIP)]

    turned = dq_t[...].T * FACTOR
    for k in range(8):
        main = turned[k * CHUNK : (k + 1) * CHUNK]
        rest = turned[8 * CHUNK + k * REST : 8 * CHUNK + (k + 1) * REST]
        second = jnp.concatenate([main[HALF:], rest], axis=0)
        qo[k] = (main[:HALF] + swap(second)).astype(BF)
    q_part[core, 0] = qo[mq * 2 + core]
    d_out = [
        push(qo.at[q_slot(o) * 2 + p], q_part.at[core, ring(o)], d_send.at[2 * o + p],
             d_recv.at[core, ring(o)], (q_peer(o) + p, c))
        for o in (2, 1, 3) for p in range(2)
    ]
    d_out.append(
        push(qo.at[mq * 2 + other], q_part.at[core, 0], d_send.at[0], d_recv.at[core, 0],
             (r + 1 - 2 * core, c))
    )
    for copy in d_out:
        copy.start()

    def arrive(src, dst, send, recv, peer):
        push(src, dst.at[other, 0], send.at[0], recv.at[other, 0],
             (r + 1 - 2 * core, c)).wait_recv()
        for o in range(1, 4):
            for p in range(2):
                push(src, dst.at[p, o], send.at[0], recv.at[p, o], (peer(o) + p, c)).wait_recv()

    arrive(kvo.at[pl.ds(0, STRIP)], kv_part, p_send, p_recv, k_peer)
    arrive(qo.at[0], q_part, d_send, d_recv, q_peer)
    kv0, kv1 = [
        kv_part[p, 0].astype(F32) + kv_part[p, 1].astype(F32)
        + kv_part[p, 2].astype(F32) + kv_part[p, 3].astype(F32)
        for p in range(2)
    ]
    q0, q1 = [
        q_part[p, 0].astype(F32) + q_part[p, 1].astype(F32)
        + q_part[p, 2].astype(F32) + q_part[p, 3].astype(F32)
        for p in range(2)
    ]
    dq_top = jnp.where(lanes, q0, swap(q1))
    dq_bottom = jnp.where(lanes, swap(q0), q1)
    dk = jnp.where(lanes_strip, kv0, swap(kv1)).astype(BF)
    dv = jnp.where(lanes_strip, swap(kv0), kv1).astype(BF)
    dq = jnp.concatenate([dq_top, dq_bottom], axis=0).astype(BF)

    projected = jnp.zeros((STRIP, C), F32)
    for kind, grad in enumerate((dq, dk, dv)):
        at = pl.multiple_of(kind * C + lax.rem(c, 2) * 128, 128)
        projected = projected + dot_nt(grad, iw[:, pl.ds(at, 128)])
    projected = projected.astype(BF)
    projected = jnp.concatenate([projected[:, :128], projected[:, 128:]], axis=0)
    g_s[...] = dot(sel_back[...], projected).astype(BF).reshape(N_COL, MSG, 128)
    b_out, b_in = exchange(g_s, g_r, b_send, b_recv)
    for copy in b_in:
        copy.wait_recv()
    sums = dot(sel_got[...], g_r[...].reshape(N_COL * MSG, 128))
    rows = TILE * SAMPLES
    total = gz_keep[...] + jnp.concatenate([sums[:rows], sums[rows:]], axis=1)
    out[...] = total.astype(BF)

    for copy in halos + kv_out + q_out + a_out + o_out + t_out + b_out:
        copy.wait_send()
    for copy in d_out:
        copy.wait_send()
    for k in range(8):

        @pl.when(k != mine)
        def _():
            part_copy(k).wait_send()


def shards(
    pre_silu, out_grad, query_heads, key_heads, value_heads, conv_weight, out_weight, input_weight
):
    sel = [jnp.asarray(x, BF) for x in selections()]
    turn = lambda x: jnp.transpose(x, (0, 2, 1))
    og = jnp.transpose(out_grad, (1, 2, 0, 3))
    zz = jnp.transpose(pre_silu, (1, 2, 0, 3))
    vmem = pl.BlockSpec(memory_space=pltpu.VMEM)
    dma = lambda *n: pltpu.SemaphoreType.DMA(n)
    result = pl.pallas_call(
        kernel,
        out_shape=jax.ShapeDtypeStruct((TILE * SAMPLES, C), BF),
        in_specs=[vmem] * 12,
        out_specs=vmem,
        scratch_shapes=[
            pltpu.VMEM((TR + 2, TC + 2, SAMPLES, C), BF),
            pltpu.VMEM((TILE * SAMPLES, C), F32),
            pltpu.VMEM((N_COL, PAD, 128), BF),
            pltpu.VMEM((N_COL, PAD, 128), BF),
            pltpu.VMEM((2, HALF, 128), BF),
            pltpu.VMEM((2, HALF, 128), BF),
            pltpu.VMEM((2, STRIP, 128), BF),
            pltpu.VMEM((8, HALF, 128), BF),
            pltpu.VMEM((8, HALF, 128), BF),
            pltpu.VMEM((8, STRIP, 128), BF),
            pltpu.VMEM((BLOCK, 128), BF),
            pltpu.VMEM((BLOCK, 128), BF),
            pltpu.VMEM((64, BLOCK), F32),
            pltpu.VMEM((CHUNKS, 64, CHUNK), BF),
            pltpu.VMEM((CHUNKS, 80, CHUNK), BF),
            pltpu.VMEM((64, BLOCK), F32),
            pltpu.VMEM((4, BLOCK), F32),
            pltpu.VMEM((4, 4, BLOCK), F32),
            pltpu.VMEM((BLOCK, 128), BF),
            pltpu.VMEM((2, 4, STRIP, 128), BF),
            pltpu.VMEM((128, BLOCK), F32),
            pltpu.VMEM((8, HALF, 128), BF),
            pltpu.VMEM((2, 4, HALF, 128), BF),
            pltpu.VMEM((N_COL, MSG, 128), BF),
            pltpu.VMEM((N_COL, MSG, 128), BF),
            dma(8), dma(8), dma(16), dma(16), dma(8), dma(8), dma(8), dma(8),
            dma(8), dma(8), dma(4), dma(4), dma(8), dma(2, 4), dma(8), dma(2, 4),
            dma(16), dma(16),
        ],
        compiler_params=pltpu.CompilerParams(
            collective_id=0, has_side_effects=True, vmem_limit_bytes=56 * 2**20
        ),
    )(
        og, zz, turn(query_heads), turn(key_heads), turn(value_heads), conv_weight, out_weight, input_weight,
        *sel,
    )
    return jnp.transpose(result.reshape(TR, TC, SAMPLES, C), (2, 0, 1, 3))


def solution(mesh):
    in_specs = (
        P(None, "row", "col", None),
        P(None, "row", "col", None),
        P("col", "row", None),
        P("col", "row", None),
        P("col", "row", None),
        P(),
        P(),
        P(),
    )
    out_specs = P(None, "row", "col", None)
    return jax.shard_map(shards, mesh=mesh, in_specs=in_specs, out_specs=out_specs, check_vma=False)
```

time: 103 us -> 84.5 us (0.82)
  the two profiles are of different devices: /device:TPU:4 before, /device:TPU:1 now
where the time goes in v2:
time: 84.5 us; the launch traced here: 84.1 us
  Pallas kernels  82.6 us (98%)
  local copies, waits for them, and re-layouts  1.52 us (2%)
    pallas_call x1, Pallas kernels, shards(): pl.pallas_call(kernel, out_shape=jax.ShapeDtypeStruct((TILE * SAMPLES, C)...  82.6 us

profile of v2, /device:TPU:1, one launch (start us, length us, event | category | flops | bytes accessed | tf_op | source)
XLA Modules:
  0.0 84.1 jit_solution(14453796479169189624)
XLA Ops:
  0.0 82.6 %shard_map.118 = bf16[144,256]{1,0:T(8,128)(2,1)} custom-call(bf16[3,6,8,256]{3,2,1,0:T(8,128)(2,1)} %bitcast.12, bf16[3,6,8,256]{3,2,1,0:T(8,128)(2,1)} %bitcast.13, bf16[2,64,288]{2,1,0:T(8,128)(2,1)} %bitcast.9, bf16[2,64,288]{2,1,0:T(8,128)(2,1)} %bitcast.10, bf16[2,64,288]{2,1,0:T(8,128)(2,1)} %bitcast.11, bf16[3,3,256,256]{3,2,1,0:T(8,128)(2,1)} %cw.1, ...), custom_call_target="tpu_custom_call" | custom-call | tf_op jit(solution)/shard_map/pallas_call | solution.py:433
  82.6 1.5 %copy.14 = bf16[8,3,6,256]{3,0,2,1:T(8,128)(2,1)} copy(bf16[8,3,6,256]{3,0,2,1:T(8,128)(2,1)} %bitcast.8) | data formatting | bytes 147456

commit v3 on v2

v3 whole, which is shorter than its diff:
```python
import functools

import jax
import jax.numpy as jnp
import numpy as np
from jax import lax
from jax.experimental import pallas as pl
from jax.experimental.pallas import tpu as pltpu
from jax.sharding import PartitionSpec as P

BF = jnp.bfloat16
F32 = jnp.float32
SAMPLES, HEADS, HD, C = 8, 4, 64, 256
TR, TC = 3, 6
N_ROW, N_COL = 32, 16
WID = TC * N_COL
STRIP = TR * WID
HALF = STRIP // 2
BLOCK = 8 * STRIP
CHUNK = 256
CHUNKS = BLOCK // CHUNK
PAD = 24
TILE = TR * TC
MESH = pl.DeviceIdType.MESH
FACTOR = HD**-0.5
LOG2E = float(np.log2(np.e))
KAPPA = FACTOR * LOG2E
NT = (((1,), (1,)), ((), ()))


PART_A = 128
PART_B = STRIP - PART_A
HALF_A, HALF_B = PART_A // 2, PART_B // 2
LEN_A = 8 * PART_A
LEN_B = 8 * PART_B
MSG = 40


def selections():
    tile = np.zeros((SAMPLES * PAD, TILE * SAMPLES), np.float32)
    strip = np.zeros((STRIP, N_COL * PAD), np.float32)
    back = np.zeros((N_COL * MSG, 2 * STRIP), np.float32)
    got = np.zeros((2 * TILE * SAMPLES, N_COL * MSG), np.float32)
    got_q = np.zeros((2 * TILE * SAMPLES, N_COL * PAD), np.float32)
    for t in range(TILE):
        for s in range(SAMPLES):
            tile[s * PAD + t, t * SAMPLES + s] = 1.0
        for n in range(N_COL):
            place = (t // TC) * WID + n * TC + t % TC
            strip[place, n * PAD + t] = 1.0
            row = t * SAMPLES + n // 2
            got_q[(n % 2) * TILE * SAMPLES + row, n * PAD + t] = 1.0
            for half in range(2):
                back[n * MSG + half * TILE + t, half * STRIP + place] = 1.0
                got[half * TILE * SAMPLES + row, n * MSG + half * TILE + t] = 1.0
    return tile, strip, back, got, strip.T, got_q


def dot(a, b):
    return jnp.dot(a, b, preferred_element_type=F32)


def dot_nt(a, b):
    return lax.dot_general(a, b, NT, preferred_element_type=F32)


def swap(x):
    return pltpu.roll(x, 64, 1)


def kernel(
    og, zz, qh, kh, vh, eye, *refs,
):
    (
        hbm_cw, hbm_ow, hbm_iw, hbm_tile, hbm_strip, hbm_back, hbm_got, hbm_back_q, hbm_got_q,
        out,
        cw, ow, iw, sel_tile, sel_strip, sel_back, sel_got, sel_back_q, sel_got_q, load_sem,
        xp, gz_keep, ga_s, do_r, qpk, opk, kvpk, q_r, o_r, kv_r, qz, oz, k_t, v_t1,
        o_t, e_s, st_s, lse_s, lse_r, rd_s, rd_r, kv_acc, kvo, kv_part, dq_t, qa, qb,
        qa_part, qb_part, g_s, g_r, h_s, h_r,
        halo_send, halo_recv, a_send, a_recv, q_send, q_recv, o_send, o_recv,
        k_send, k_recv, l_send, l_recv, t_send, t_recv, p_send, p_recv, d_send, d_recv,
        e_send, e_recv, b_send, b_recv, h_send, h_recv,
    ) = refs
    r = lax.axis_index("row")
    c = lax.axis_index("col")
    loads = [
        pltpu.make_async_copy(src, dst, load_sem.at[n])
        for n, (src, dst) in enumerate(
            [(hbm_cw, cw), (hbm_tile, sel_tile), (hbm_ow, ow), (hbm_strip, sel_strip),
             (hbm_iw, iw), (hbm_back, sel_back), (hbm_got, sel_got),
             (hbm_back_q, sel_back_q), (hbm_got_q, sel_got_q)]
        )
    ]
    core = lax.rem(r, 2)
    other = 1 - core
    zi = lax.rem(r // 2, 8)
    xh = r // 16
    zl = lax.rem(zi, 2)
    mq = zi // 2

    def q_peer(o):
        return xh * 16 + (2 * lax.rem(mq + o, 4) + zl) * 2

    def k_peer(o):
        return lax.rem(xh + o // 2, 2) * 16 + (2 * mq + lax.rem(zl + lax.rem(o, 2), 2)) * 2

    def wrap(x, n):
        return lax.rem(x + n, n)

    lanes = lax.broadcasted_iota(jnp.int32, (HALF, 128), 1) < 64
    lanes_strip = lax.broadcasted_iota(jnp.int32, (STRIP, 128), 1) < 64
    lanes_chunk = lax.broadcasted_iota(jnp.int32, (CHUNK, 128), 1) < 64

    barrier = pltpu.get_barrier_semaphore()
    shifts = [(i, j) for i in (-1, 0, 1) for j in (-1, 0, 1) if (i, j) != (0, 0)]
    peers = [(wrap(r + i, N_ROW), wrap(c + j, N_COL)) for i, j in shifts]
    peers += [(r, lax.rem(c + o, N_COL)) for o in range(2, N_COL - 1)]
    for peer in (q_peer, k_peer):
        for o in range(1, 4):
            peers += [(peer(o), c), (peer(o) + 1, c)]
    peers += [(r + 1 - 2 * core, c)]
    for peer in peers:
        pl.semaphore_signal(barrier, inc=1, device_id=peer, device_id_type=MESH)

    for load in loads:
        load.start()

    def halves(x, dst):
        top = jnp.concatenate([x[:HALF_A], x[PART_A : PART_A + HALF_B]], axis=0)
        bottom = jnp.concatenate([x[HALF_A:PART_A], x[PART_A + HALF_B :]], axis=0)
        dst[0] = jnp.where(lanes, top, swap(bottom)).astype(BF)
        dst[1] = jnp.where(lanes, swap(top), bottom).astype(BF)

    for p in range(2):
        kvpk[p] = jnp.concatenate([kh[p], vh[p]], axis=0).T
    halves(jnp.concatenate([qh[0], qh[1]], axis=0).T.astype(F32), qpk)
    xp[1:4, 1:7] = og[...]
    pl.semaphore_wait(barrier, len(peers))

    def push(src, dst, send, recv, peer):
        copy = pltpu.make_async_remote_copy(
            src_ref=src, dst_ref=dst, send_sem=send, recv_sem=recv,
            device_id=peer, device_id_type=MESH,
        )
        return copy

    def rim(shift, width, take):
        if shift == 0:
            return pl.ds(0, width) if take else pl.ds(1, width)
        if take:
            return pl.ds(width - 1, 1) if shift == 1 else pl.ds(0, 1)
        return pl.ds(0, 1) if shift == 1 else pl.ds(width + 1, 1)

    halos = []
    for index, (i, j) in enumerate(shifts):
        halos.append(
            push(
                og.at[rim(i, TR, True), rim(j, TC, True)],
                xp.at[rim(i, TR, False), rim(j, TC, False)],
                halo_send.at[index], halo_recv.at[index],
                (wrap(r + i, N_ROW), wrap(c + j, N_COL)),
            )
        )
    for copy in halos:
        copy.start()

    def gather(src, dst, peer, slot, turn, order, send, recv):
        here = (r + 1 - 2 * core, c)
        dst[slot(0) * 2 + core] = src[core]
        started = [
            push(src.at[other], dst.at[slot(0) * 2 + core], send.at[0], recv.at[0], here)
        ]
        arrivals = {
            0: [push(src.at[0], dst.at[slot(0) * 2 + other], send.at[0], recv.at[0], here)]
        }
        for o in order:
            there = turn(o)
            arrivals[o] = []
            for p in range(2):
                started.append(
                    push(src.at[p], dst.at[slot(o, True) * 2 + core], send.at[2 * o + p],
                         recv.at[2 * there + core], (peer(o) + p, c))
                )
                arrivals[o].append(
                    push(src.at[p], dst.at[slot(o) * 2 + p], send.at[2 * o + p],
                         recv.at[2 * o + p], (peer(o) + p, c))
                )
        return started, arrivals

    def k_slot(o, remote=False):
        return 3 - o

    def q_slot(o, remote=False):
        return mq if remote else lax.rem(mq + o, 4)

    ring = lambda o: (4 - o) % 4
    kv_out, kv_in = gather(kvpk, kv_r, k_peer, k_slot, lambda o: o, (1, 2, 3), k_send, k_recv)
    q_out, q_in = gather(qpk, q_r, q_peer, q_slot, ring, (1, 3, 2), q_send, q_recv)
    for copy in kv_out + q_out[:1]:
        copy.start()

    for load in loads[:3]:
        load.wait()

    for copy in halos:
        copy.wait_recv()
    zero_row = jnp.zeros((1, TC + 2, SAMPLES, C), BF)
    zero_col = jnp.zeros((TR + 2, 1, SAMPLES, C), BF)

    @pl.when(r == 0)
    def _():
        xp[0:1] = zero_row

    @pl.when(r == N_ROW - 1)
    def _():
        xp[TR + 1 : TR + 2] = zero_row

    @pl.when(c == 0)
    def _():
        xp[:, 0:1] = zero_col

    @pl.when(c == N_COL - 1)
    def _():
        xp[:, TC + 1 : TC + 2] = zero_col

    cells = xp[...].astype(F32)
    conv = jnp.zeros((TILE * SAMPLES, C), F32)
    for a in (-1, 0, 1):
        for b in (-1, 0, 1):
            window = cells[1 - a : 1 - a + TR, 1 - b : 1 - b + TC]
            window = window.reshape(TILE * SAMPLES, C).astype(BF)
            conv = conv + dot_nt(window, cw[a + 1, b + 1])
    z = zz[...].astype(F32).reshape(TILE * SAMPLES, C)
    sig = jax.nn.sigmoid(z)
    grad_z = (conv * sig * (1.0 + z * (1.0 - sig))).astype(BF)
    gz_keep[...] = grad_z.astype(F32)
    placed = dot(sel_tile[...], grad_z)
    ga = dot_nt(placed.astype(BF), ow[...])
    for s in range(SAMPLES):
        for b in range(2):
            piece = ga[s * PAD : (s + 1) * PAD, b * 128 : (b + 1) * 128]
            ga_s[2 * s + b] = piece.reshape(3, 8, 128).astype(BF)

    def flat(ref, rows):
        return ref[...].astype(F32).reshape(rows, 128).astype(BF)

    def exchange(src, dst, send, recv):
        dst[c] = src[c]
        started, arrivals = [], []
        for o in range(1, N_COL):
            to, back = lax.rem(c + o, N_COL), lax.rem(c + N_COL - o, N_COL)
            started.append(push(src.at[to], dst.at[c], send.at[o], recv.at[o], (r, to)))
            arrivals.append(
                push(src.at[back], dst.at[back], send.at[o], recv.at[o], (r, back))
            )
        for copy in started:
            copy.start()
        return started, arrivals

    a_out, a_in = exchange(ga_s, do_r, a_send, a_recv)
    for copy in q_out[1:]:
        copy.start()

    def unpack(src, slot, dst, left):
        x = src[slot].astype(F32)
        if left:
            top, bottom = jnp.where(lanes, x, 0.0), jnp.where(lanes, swap(x), 0.0)
        else:
            top, bottom = jnp.where(lanes, 0.0, swap(x)), jnp.where(lanes, 0.0, x)
        top, bottom = top.astype(BF), bottom.astype(BF)
        at = pl.multiple_of(slot * PART_A, PART_A)
        dst[pl.ds(at, HALF_A)] = top[:HALF_A]
        dst[pl.ds(at + HALF_A, HALF_A)] = bottom[:HALF_A]
        at = pl.multiple_of(LEN_A + slot * PART_B, 32)
        dst[pl.ds(at, HALF_B)] = top[HALF_A:]
        dst[pl.ds(at + HALF_B, HALF_B)] = bottom[HALF_A:]

    for o in range(4):
        for copy in kv_in[o]:
            copy.wait_recv()
    keys = kv_r.reshape(BLOCK, 128)
    v_t1[:, 64:80, :] = jnp.ones((CHUNKS, 16, CHUNK), BF)
    for k in range(CHUNKS):
        turned = dot_nt(eye[...], keys[k * CHUNK : (k + 1) * CHUNK]).astype(BF)
        k_t[k] = turned[:64]
        v_t1[k, 0:64, :] = turned[64:]

    def stats_chunk(at):
        scores = dot_nt(keys[...], qz[pl.ds(at, CHUNK)])
        top = jnp.max(scores, axis=0, keepdims=True) * KAPPA
        e = jnp.exp2(scores * KAPPA - top)
        st_s[0:1, pl.ds(at, CHUNK)] = top
        st_s[1:2, pl.ds(at, CHUNK)] = jnp.sum(e, axis=0, keepdims=True)
        eb = e.astype(BF)
        e_s[:, pl.ds(at, CHUNK)] = eb
        acc = jnp.zeros((80, CHUNK), F32)
        for k in range(CHUNKS):
            acc = acc + dot(v_t1[k], eb[k * CHUNK : (k + 1) * CHUNK])
        st_s[2:3, pl.ds(at, CHUNK)] = acc[64:65]
        o_t[:, pl.ds(at, CHUNK)] = acc[:64]

    def stats_member(o):
        for copy in q_in[o]:
            copy.wait_recv()

        for k in range(2):
            unpack(q_r, q_slot(o) * 2 + k, qz, True)
        return o

    def stats_part(o):
        stats_chunk(pl.multiple_of(q_slot(o) * CHUNK, CHUNK))

    stats_part(stats_member(0))
    for copy in a_in:
        copy.wait_recv()
    for load in loads[3:]:
        load.wait()
    halves(dot(sel_strip[...], flat(do_r, N_COL * PAD)), opk)
    o_out, o_in = gather(opk, o_r, q_peer, q_slot, ring, (1, 3, 2), o_send, o_recv)
    for copy in o_out:
        copy.start()
    for o in (1, 3, 2):
        stats_part(stats_member(o))

    def stats_step(k, carry):
        stats_chunk(pl.multiple_of(LEN_A + k * CHUNK, CHUNK))
        return carry

    lax.fori_loop(0, LEN_B // CHUNK, stats_step, 0)

    def share(src, dst, send, recv):
        dst[0] = src[...]
        started, arrivals = [], []
        for o in (2, 1, 3):
            peer = (q_peer(o) + core, c)
            started.append(push(src, dst.at[ring(o)], send.at[o], recv.at[ring(o)], peer))
            arrivals.append(push(src, dst.at[o], send.at[o], recv.at[o], peer))
        for copy in started:
            copy.start()
        return started, arrivals

    lse_s[...] = st_s[0:1] + jnp.log(st_s[1:2]) * LOG2E
    l_out, l_in = share(lse_s, lse_r, l_send, l_recv)
    for o in range(4):
        for copy in o_in[o]:
            copy.wait_recv()
    for k in range(8):
        unpack(o_r, k, oz, False)
    do_t = dot_nt(eye[64:], oz[...])
    rd_s[...] = jnp.sum(o_t[...] * do_t, axis=0, keepdims=True) / st_s[2:3]
    t_out, t_in = share(rd_s, rd_r, t_send, t_recv)
    for copy in l_in:
        copy.wait_recv()
    logs = [lse_r[n] for n in range(4)]
    top = jnp.maximum(jnp.maximum(logs[0], logs[1]), jnp.maximum(logs[2], logs[3]))
    norm = sum(jnp.exp2(log - top) for log in logs)
    log_norm = top + jnp.log(norm) * LOG2E
    rescale = jnp.exp2(st_s[0:1] - log_norm)
    shares = [jnp.exp2(log - log_norm) for log in logs]
    for copy in t_in:
        copy.wait_recv()
    row_dot = sum(share * rd_r[n] for n, share in enumerate(shares))

    dq_t[...] = jnp.zeros_like(dq_t)
    mine = 6 + core

    def part_copy(k):
        at = pl.multiple_of(k * STRIP, 32)
        o = 3 - k // 2
        return push(
            kvo.at[pl.ds(at, STRIP)], kv_part.at[core, o], p_send.at[k],
            p_recv.at[core, o], (k_peer(o) + lax.rem(k, 2), c),
        )

    def grad_pass(lo, width, last):
        part = slice(lo, lo + width)

        def step(j, carry):
            at = pl.multiple_of(j * CHUNK, CHUNK)
            probs = e_s[pl.ds(at, CHUNK), part].astype(F32) * rescale[:, part]
            grad_probs = dot_nt(keys[pl.ds(at, CHUNK)], oz[part])
            grad_scores = (probs * (grad_probs - row_dot[:, part])).astype(BF)
            both = dot(grad_scores, qz[part]) + dot(probs.astype(BF), oz[part])
            dq_t[0:64, part] += dot(k_t[j], grad_scores)
            if not last:
                kv_acc[pl.ds(at, CHUNK)] = both
                return carry
            both = both + kv_acc[pl.ds(at, CHUNK)]
            kvo[pl.ds(at, CHUNK)] = jnp.where(lanes_chunk, both * FACTOR, both).astype(BF)
            k = j - 1

            @pl.when(jnp.logical_and(k >= 0, k != mine))
            def _():
                part_copy(k).start()

            return carry

        lax.fori_loop(0, CHUNKS, step, 0)

    def send_queries(part, half, src, dst, send, recv):
        turned = dq_t[:, part].T * FACTOR
        for k in range(8):
            first = turned[2 * k * half : (2 * k + 1) * half]
            second = turned[(2 * k + 1) * half : (2 * k + 2) * half]
            src[k] = (first + swap(second)).astype(BF)
        dst[core, 0] = src[mq * 2 + core]
        started = [
            push(src.at[q_slot(o) * 2 + p], dst.at[core, ring(o)], send.at[2 * o + p],
                 recv.at[core, ring(o)], (q_peer(o) + p, c))
            for o in (2, 1, 3) for p in range(2)
        ]
        started.append(
            push(src.at[mq * 2 + other], dst.at[core, 0], send.at[0], recv.at[core, 0],
                 (r + 1 - 2 * core, c))
        )
        for copy in started:
            copy.start()
        return started

    grad_pass(LEN_A, LEN_B, False)
    d_out = send_queries(slice(LEN_A, BLOCK), HALF_B, qb, qb_part, d_send, d_recv)
    grad_pass(0, LEN_A, True)
    kv_part[core, 0] = kvo[pl.ds(pl.multiple_of(mine * STRIP, 32), STRIP)]
    d_out += send_queries(slice(0, LEN_A), HALF_A, qa, qa_part, e_send, e_recv)

    def arrive(src, dst, send, recv, peer):
        push(src, dst.at[other, 0], send.at[0], recv.at[other, 0],
             (r + 1 - 2 * core, c)).wait_recv()
        for o in range(1, 4):
            for p in range(2):
                push(src, dst.at[p, o], send.at[0], recv.at[p, o], (peer(o) + p, c)).wait_recv()

    arrive(kvo.at[pl.ds(0, STRIP)], kv_part, p_send, p_recv, k_peer)
    kv0, kv1 = [sum(kv_part[p, n].astype(F32) for n in range(4)) for p in range(2)]
    dk = jnp.where(lanes_strip, kv0, swap(kv1)).astype(BF)
    dv = jnp.where(lanes_strip, swap(kv0), kv1).astype(BF)

    def weight(kind):
        return iw[:, pl.ds(pl.multiple_of(kind * C + lax.rem(c, 2) * 128, 128), 128)]

    projected = (dot_nt(dk, weight(1)) + dot_nt(dv, weight(2))).astype(BF)
    projected = jnp.concatenate([projected[:, :128], projected[:, 128:]], axis=0)
    placed = dot(sel_back[...], projected)
    g_s[...] = placed.reshape(N_COL, MSG // 8, 8, 128).astype(BF)
    b_out, b_in = exchange(g_s, g_r, b_send, b_recv)

    arrive(qb.at[0], qb_part, d_send, d_recv, q_peer)
    arrive(qa.at[0], qa_part, e_send, e_recv, q_peer)

    def unpacked(part, keep):
        q0, q1 = [sum(part[p, n].astype(F32) for n in range(4)) for p in range(2)]
        return [jnp.where(keep, q0, swap(q1)), jnp.where(keep, swap(q0), q1)]

    dq = unpacked(qa_part, lanes[:HALF_A]) + unpacked(qb_part, lanes[:HALF_B])
    placed = dot(sel_back_q[...], jnp.concatenate(dq, axis=0).astype(BF))
    h_s[...] = placed.reshape(N_COL, PAD // 8, 8, 128).astype(BF)
    h_out, h_in = exchange(h_s, h_r, h_send, h_recv)
    rows = TILE * SAMPLES
    for copy in b_in:
        copy.wait_recv()
    sums = dot(sel_got[...], flat(g_r, N_COL * MSG))
    total = gz_keep[...] + jnp.concatenate([sums[:rows], sums[rows:]], axis=1)
    for copy in h_in:
        copy.wait_recv()
    got = dot(sel_got_q[...], flat(h_r, N_COL * PAD)).astype(BF)
    for b in range(2):
        total = total + dot_nt(got[b * rows : (b + 1) * rows], iw[:, b * 128 : (b + 1) * 128])
    out[...] = total.astype(BF)

    for copy in halos + kv_out + q_out + a_out + o_out + l_out + t_out + b_out + h_out:
        copy.wait_send()
    for copy in d_out:
        copy.wait_send()
    for k in range(8):

        @pl.when(k != mine)
        def _():
            part_copy(k).wait_send()


def shards(
    pre_silu, out_grad, query_heads, key_heads, value_heads, conv_weight, out_weight, input_weight
):
    sel = [jnp.asarray(x, BF) for x in selections()]
    turn = lambda x: jnp.transpose(x, (0, 2, 1))
    og = jnp.transpose(out_grad, (1, 2, 0, 3))
    zz = jnp.transpose(pre_silu, (1, 2, 0, 3))
    vmem = pl.BlockSpec(memory_space=pltpu.VMEM)
    dma = lambda *n: pltpu.SemaphoreType.DMA(n)
    result = pl.pallas_call(
        kernel,
        out_shape=jax.ShapeDtypeStruct((TILE * SAMPLES, C), BF),
        in_specs=[vmem] * 6 + [pl.BlockSpec(memory_space=pl.ANY)] * 9,
        out_specs=vmem,
        scratch_shapes=[
            *[pltpu.VMEM(x.shape, BF) for x in (conv_weight, out_weight, input_weight, *sel)],
            dma(9),
            pltpu.VMEM((TR + 2, TC + 2, SAMPLES, C), BF),
            pltpu.VMEM((TILE * SAMPLES, C), F32),
            pltpu.VMEM((N_COL, PAD // 8, 8, 128), BF),
            pltpu.VMEM((N_COL, PAD // 8, 8, 128), BF),
            pltpu.VMEM((2, HALF, 128), BF),
            pltpu.VMEM((2, HALF, 128), BF),
            pltpu.VMEM((2, STRIP, 128), BF),
            pltpu.VMEM((8, HALF, 128), BF),
            pltpu.VMEM((8, HALF, 128), BF),
            pltpu.VMEM((8, STRIP, 128), BF),
            pltpu.VMEM((BLOCK, 128), BF),
            pltpu.VMEM((BLOCK, 128), BF),
            pltpu.VMEM((CHUNKS, 64, CHUNK), BF),
            pltpu.VMEM((CHUNKS, 80, CHUNK), BF),
            pltpu.VMEM((64, BLOCK), F32),
            pltpu.VMEM((BLOCK, BLOCK), BF),
            pltpu.VMEM((4, BLOCK), F32),
            pltpu.VMEM((1, BLOCK), F32),
            pltpu.VMEM((4, 1, BLOCK), F32),
            pltpu.VMEM((1, BLOCK), F32),
            pltpu.VMEM((4, 1, BLOCK), F32),
            pltpu.VMEM((BLOCK, 128), F32),
            pltpu.VMEM((BLOCK, 128), BF),
            pltpu.VMEM((2, 4, STRIP, 128), BF),
            pltpu.VMEM((128, BLOCK), F32),
            pltpu.VMEM((8, HALF_A, 128), BF),
            pltpu.VMEM((8, HALF_B, 128), BF),
            pltpu.VMEM((2, 4, HALF_A, 128), BF),
            pltpu.VMEM((2, 4, HALF_B, 128), BF),
            pltpu.VMEM((N_COL, MSG // 8, 8, 128), BF),
            pltpu.VMEM((N_COL, MSG // 8, 8, 128), BF),
            pltpu.VMEM((N_COL, PAD // 8, 8, 128), BF),
            pltpu.VMEM((N_COL, PAD // 8, 8, 128), BF),
            dma(8), dma(8), dma(16), dma(16), dma(8), dma(8), dma(8), dma(8),
            dma(8), dma(8), dma(4), dma(4), dma(4), dma(4), dma(8), dma(2, 4), dma(8), dma(2, 4),
            dma(8), dma(2, 4), dma(16), dma(16), dma(16), dma(16),
        ],
        compiler_params=pltpu.CompilerParams(
            collective_id=0, has_side_effects=True, vmem_limit_bytes=56 * 2**20
        ),
    )(
        og, zz, turn(query_heads), turn(key_heads), turn(value_heads), jnp.asarray(np.eye(128), BF),
        conv_weight, out_weight, input_weight, *sel,
    )
    return jnp.transpose(result.reshape(TR, TC, SAMPLES, C), (2, 0, 1, 3))


def solution(mesh):
    in_specs = (
        P(None, "row", "col", None),
        P(None, "row", "col", None),
        P("col", "row", None),
        P("col", "row", None),
        P("col", "row", None),
        P(),
        P(),
        P(),
    )
    out_specs = P(None, "row", "col", None)
    return jax.shard_map(shards, mesh=mesh, in_specs=in_specs, out_specs=out_specs, check_vma=False)
```

time: 84.5 us -> 83.7 us (level)
  no operation moved by 1% of the time
where the time goes in v3:
time: 83.7 us; the launch traced here: 83.5 us
  Pallas kernels  81.9 us (98%)
  local copies, waits for them, and re-layouts  1.52 us (2%)
    pallas_call x1, Pallas kernels, shards(): pl.pallas_call(kernel, out_shape=jax.ShapeDtypeStruct((TILE * SAMPLES, C)...  81.9 us

profile of v3, /device:TPU:1, one launch (start us, length us, event | category | flops | bytes accessed | tf_op | source)
XLA Modules:
  0.0 83.5 jit_solution(13877921549788593835)
XLA Ops:
  0.0 81.9 %shard_map.145 = bf16[144,256]{1,0:T(8,128)(2,1)} custom-call(bf16[3,6,8,256]{3,2,1,0:T(8,128)(2,1)} %bitcast.12, bf16[3,6,8,256]{3,2,1,0:T(8,128)(2,1)} %bitcast.13, bf16[2,64,288]{2,1,0:T(8,128)(2,1)} %bitcast.9, bf16[2,64,288]{2,1,0:T(8,128)(2,1)} %bitcast.10, bf16[2,64,288]{2,1,0:T(8,128)(2,1)} %bitcast.11, bf16[128,128]{1,0:T(8,128)(2,1)} %constant.20.clone.eye, ...), custom_call_target="tpu_custom_call" | custom-call | tf_op jit(solution)/shard_map/pallas_call | solution.py:491
  81.9 1.5 %copy.17 = bf16[8,3,6,256]{3,0,2,1:T(8,128)(2,1)} copy(bf16[8,3,6,256]{3,0,2,1:T(8,128)(2,1)} %bitcast.8) | data formatting | bytes 147456

commit v4 on v3

--- a/solution.py
+++ b/solution.py
@@ -28,7 +28,7 @@
 NT = (((1,), (1,)), ((), ()))
 
 
-PART_A = 128
+PART_A = 192
 PART_B = STRIP - PART_A
 HALF_A, HALF_B = PART_A // 2, PART_B // 2
 LEN_A = 8 * PART_A
@@ -41,7 +41,6 @@
     strip = np.zeros((STRIP, N_COL * PAD), np.float32)
     back = np.zeros((N_COL * MSG, 2 * STRIP), np.float32)
     got = np.zeros((2 * TILE * SAMPLES, N_COL * MSG), np.float32)
-    got_q = np.zeros((2 * TILE * SAMPLES, N_COL * PAD), np.float32)
     for t in range(TILE):
         for s in range(SAMPLES):
             tile[s * PAD + t, t * SAMPLES + s] = 1.0
@@ -49,11 +48,10 @@
             place = (t // TC) * WID + n * TC + t % TC
             strip[place, n * PAD + t] = 1.0
             row = t * SAMPLES + n // 2
-            got_q[(n % 2) * TILE * SAMPLES + row, n * PAD + t] = 1.0
             for half in range(2):
                 back[n * MSG + half * TILE + t, half * STRIP + place] = 1.0
                 got[half * TILE * SAMPLES + row, n * MSG + half * TILE + t] = 1.0
-    return tile, strip, back, got, strip.T, got_q
+    return tile, strip, back, got
 
 
 def dot(a, b):
@@ -62,6 +60,10 @@
 
 def dot_nt(a, b):
     return lax.dot_general(a, b, NT, preferred_element_type=F32)
+
+
+def dot_tn(a, b):
+    return lax.dot_general(a, b, (((0,), (0,)), ((), ())), preferred_element_type=F32)
 
 
 def swap(x):
@@ -72,9 +74,9 @@
     og, zz, qh, kh, vh, eye, *refs,
 ):
     (
-        hbm_cw, hbm_ow, hbm_iw, hbm_tile, hbm_strip, hbm_back, hbm_got, hbm_back_q, hbm_got_q,
+        hbm_cw, hbm_ow, hbm_iw, hbm_tile, hbm_strip, hbm_back, hbm_got,
         out,
-        cw, ow, iw, sel_tile, sel_strip, sel_back, sel_got, sel_back_q, sel_got_q, load_sem,
+        cw, ow, iw, sel_tile, sel_strip, sel_back, sel_got, load_sem,
         xp, gz_keep, ga_s, do_r, qpk, opk, kvpk, q_r, o_r, kv_r, qz, oz, k_t, v_t1,
         o_t, e_s, st_s, lse_s, lse_r, rd_s, rd_r, kv_acc, kvo, kv_part, dq_t, qa, qb,
         qa_part, qb_part, g_s, g_r, h_s, h_r,
@@ -88,8 +90,7 @@
         pltpu.make_async_copy(src, dst, load_sem.at[n])
         for n, (src, dst) in enumerate(
             [(hbm_cw, cw), (hbm_tile, sel_tile), (hbm_ow, ow), (hbm_strip, sel_strip),
-             (hbm_iw, iw), (hbm_back, sel_back), (hbm_got, sel_got),
-             (hbm_back_q, sel_back_q), (hbm_got_q, sel_got_q)]
+             (hbm_iw, iw), (hbm_back, sel_back), (hbm_got, sel_got)]
         )
     ]
     core = lax.rem(r, 2)
@@ -286,19 +287,20 @@
         k_t[k] = turned[:64]
         v_t1[k, 0:64, :] = turned[64:]
 
-    def stats_chunk(at):
-        scores = dot_nt(keys[...], qz[pl.ds(at, CHUNK)])
+    def stats_chunk(at, width):
+        here = pl.ds(at, width)
+        scores = dot_nt(keys[...], qz[here])
         top = jnp.max(scores, axis=0, keepdims=True) * KAPPA
         e = jnp.exp2(scores * KAPPA - top)
-        st_s[0:1, pl.ds(at, CHUNK)] = top
-        st_s[1:2, pl.ds(at, CHUNK)] = jnp.sum(e, axis=0, keepdims=True)
+        st_s[0:1, here] = top
+        st_s[1:2, here] = jnp.sum(e, axis=0, keepdims=True)
         eb = e.astype(BF)
-        e_s[:, pl.ds(at, CHUNK)] = eb
-        acc = jnp.zeros((80, CHUNK), F32)
+        e_s[:, here] = eb
+        acc = jnp.zeros((80, width), F32)
         for k in range(CHUNKS):
             acc = acc + dot(v_t1[k], eb[k * CHUNK : (k + 1) * CHUNK])
-        st_s[2:3, pl.ds(at, CHUNK)] = acc[64:65]
-        o_t[:, pl.ds(at, CHUNK)] = acc[:64]
+        st_s[2:3, here] = acc[64:65]
+        o_t[:, here] = acc[:64]
 
     def stats_member(o):
         for copy in q_in[o]:
@@ -309,7 +311,7 @@
         return o
 
     def stats_part(o):
-        stats_chunk(pl.multiple_of(q_slot(o) * CHUNK, CHUNK))
+        stats_chunk(pl.multiple_of(q_slot(o) * 2 * PART_A, 128), 2 * PART_A)
 
     stats_part(stats_member(0))
     for copy in a_in:
@@ -323,11 +325,7 @@
     for o in (1, 3, 2):
         stats_part(stats_member(o))
 
-    def stats_step(k, carry):
-        stats_chunk(pl.multiple_of(LEN_A + k * CHUNK, CHUNK))
-        return carry
-
-    lax.fori_loop(0, LEN_B // CHUNK, stats_step, 0)
+    stats_chunk(LEN_A, LEN_B)
 
     def share(src, dst, send, recv):
         dst[0] = src[...]
@@ -396,7 +394,7 @@
 
             return carry
 
-        lax.fori_loop(0, CHUNKS, step, 0)
+        lax.fori_loop(0, CHUNKS, step, 0, unroll=3)
 
     def send_queries(part, half, src, dst, send, recv):
         turned = dq_t[:, part].T * FACTOR
@@ -418,11 +416,11 @@
             copy.start()
         return started
 
-    grad_pass(LEN_A, LEN_B, False)
-    d_out = send_queries(slice(LEN_A, BLOCK), HALF_B, qb, qb_part, d_send, d_recv)
-    grad_pass(0, LEN_A, True)
+    grad_pass(0, LEN_A, False)
+    d_out = send_queries(slice(0, LEN_A), HALF_A, qa, qa_part, d_send, d_recv)
+    grad_pass(LEN_A, LEN_B, True)
     kv_part[core, 0] = kvo[pl.ds(pl.multiple_of(mine * STRIP, 32), STRIP)]
-    d_out += send_queries(slice(0, LEN_A), HALF_A, qa, qa_part, e_send, e_recv)
+    d_out += send_queries(slice(LEN_A, BLOCK), HALF_B, qb, qb_part, e_send, e_recv)
 
     def arrive(src, dst, send, recv, peer):
         push(src, dst.at[other, 0], send.at[0], recv.at[other, 0],
@@ -445,15 +443,15 @@
     g_s[...] = placed.reshape(N_COL, MSG // 8, 8, 128).astype(BF)
     b_out, b_in = exchange(g_s, g_r, b_send, b_recv)
 
-    arrive(qb.at[0], qb_part, d_send, d_recv, q_peer)
-    arrive(qa.at[0], qa_part, e_send, e_recv, q_peer)
+    arrive(qa.at[0], qa_part, d_send, d_recv, q_peer)
+    arrive(qb.at[0], qb_part, e_send, e_recv, q_peer)
 
     def unpacked(part, keep):
         q0, q1 = [sum(part[p, n].astype(F32) for n in range(4)) for p in range(2)]
         return [jnp.where(keep, q0, swap(q1)), jnp.where(keep, swap(q0), q1)]
 
     dq = unpacked(qa_part, lanes[:HALF_A]) + unpacked(qb_part, lanes[:HALF_B])
-    placed = dot(sel_back_q[...], jnp.concatenate(dq, axis=0).astype(BF))
+    placed = dot_tn(sel_strip[...], jnp.concatenate(dq, axis=0).astype(BF))
     h_s[...] = placed.reshape(N_COL, PAD // 8, 8, 128).astype(BF)
     h_out, h_in = exchange(h_s, h_r, h_send, h_recv)
     rows = TILE * SAMPLES
@@ -463,9 +461,10 @@
     total = gz_keep[...] + jnp.concatenate([sums[:rows], sums[rows:]], axis=1)
     for copy in h_in:
         copy.wait_recv()
-    got = dot(sel_got_q[...], flat(h_r, N_COL * PAD)).astype(BF)
     for b in range(2):
-        total = total + dot_nt(got[b * rows : (b + 1) * rows], iw[:, b * 128 : (b + 1) * 128])
+        got = jnp.concatenate([h_r[2 * s + b].astype(F32) for s in range(SAMPLES)], axis=0)
+        got = dot_tn(sel_tile[...], got.reshape(SAMPLES * PAD, 128).astype(BF)).astype(BF)
+        total = total + dot_nt(got, iw[:, b * 128 : (b + 1) * 128])
     out[...] = total.astype(BF)
 
     for copy in halos + kv_out + q_out + a_out + o_out + l_out + t_out + b_out + h_out:
@@ -491,11 +490,11 @@
     result = pl.pallas_call(
         kernel,
         out_shape=jax.ShapeDtypeStruct((TILE * SAMPLES, C), BF),
-        in_specs=[vmem] * 6 + [pl.BlockSpec(memory_space=pl.ANY)] * 9,
+        in_specs=[vmem] * 6 + [pl.BlockSpec(memory_space=pl.ANY)] * 7,
         out_specs=vmem,
         scratch_shapes=[
             *[pltpu.VMEM(x.shape, BF) for x in (conv_weight, out_weight, input_weight, *sel)],
-            dma(9),
+            dma(7),
             pltpu.VMEM((TR + 2, TC + 2, SAMPLES, C), BF),
             pltpu.VMEM((TILE * SAMPLES, C), F32),
             pltpu.VMEM((N_COL, PAD // 8, 8, 128), BF),

time: 83.7 us -> 79.9 us (0.955)
  Pallas kernels: 81.9 us -> 78.2 us
    pallas_call x1, Pallas kernels: 81.9 us -> 78.2 us  [shards(): pl.pallas_call(kernel, out_shape=jax.ShapeDtypeStruct((TILE * SAMPLES, C)...]
where the time goes in v4:
time: 79.9 us; the launch traced here: 79.7 us
  Pallas kernels  78.2 us (98%)
  local copies, waits for them, and re-layouts  1.52 us (2%)
    pallas_call x1, Pallas kernels, shards(): pl.pallas_call(kernel, out_shape=jax.ShapeDtypeStruct((TILE * SAMPLES, C)...  78.2 us

profile of v4, /device:TPU:1, one launch (start us, length us, event | category | flops | bytes accessed | tf_op | source)
XLA Modules:
  0.0 79.7 jit_solution(3881311530886947685)
XLA Ops:
  0.0 78.2 %shard_map.127 = bf16[144,256]{1,0:T(8,128)(2,1)} custom-call(bf16[3,6,8,256]{3,2,1,0:T(8,128)(2,1)} %bitcast.12, bf16[3,6,8,256]{3,2,1,0:T(8,128)(2,1)} %bitcast.13, bf16[2,64,288]{2,1,0:T(8,128)(2,1)} %bitcast.9, bf16[2,64,288]{2,1,0:T(8,128)(2,1)} %bitcast.10, bf16[2,64,288]{2,1,0:T(8,128)(2,1)} %bitcast.11, bf16[128,128]{1,0:T(8,128)(2,1)} %constant.14.clone.eye, ...), custom_call_target="tpu_custom_call" | custom-call | tf_op jit(solution)/shard_map/pallas_call | solution.py:490
  78.2 1.5 %copy.15 = bf16[8,3,6,256]{3,0,2,1:T(8,128)(2,1)} copy(bf16[8,3,6,256]{3,0,2,1:T(8,128)(2,1)} %bitcast.8) | data formatting | bytes 147456

commit v5 on v4

--- a/solution.py
+++ b/solution.py
@@ -198,7 +198,7 @@
     ring = lambda o: (4 - o) % 4
     kv_out, kv_in = gather(kvpk, kv_r, k_peer, k_slot, lambda o: o, (1, 2, 3), k_send, k_recv)
     q_out, q_in = gather(qpk, q_r, q_peer, q_slot, ring, (1, 3, 2), q_send, q_recv)
-    for copy in kv_out + q_out[:1]:
+    for copy in kv_out + q_out[:5]:
         copy.start()
 
     for load in loads[:3]:
@@ -260,7 +260,7 @@
         return started, arrivals
 
     a_out, a_in = exchange(ga_s, do_r, a_send, a_recv)
-    for copy in q_out[1:]:
+    for copy in q_out[5:]:
         copy.start()
 
     def unpack(src, slot, dst, left):
@@ -286,6 +286,15 @@
         turned = dot_nt(eye[...], keys[k * CHUNK : (k + 1) * CHUNK]).astype(BF)
         k_t[k] = turned[:64]
         v_t1[k, 0:64, :] = turned[64:]
+
+    for copy in a_in:
+        copy.wait_recv()
+    for load in loads[3:]:
+        load.wait()
+    halves(dot(sel_strip[...], flat(do_r, N_COL * PAD)), opk)
+    o_out, o_in = gather(opk, o_r, q_peer, q_slot, ring, (1, 3, 2), o_send, o_recv)
+    for copy in o_out:
+        copy.start()
 
     def stats_chunk(at, width):
         here = pl.ds(at, width)
@@ -313,16 +322,7 @@
     def stats_part(o):
         stats_chunk(pl.multiple_of(q_slot(o) * 2 * PART_A, 128), 2 * PART_A)
 
-    stats_part(stats_member(0))
-    for copy in a_in:
-        copy.wait_recv()
-    for load in loads[3:]:
-        load.wait()
-    halves(dot(sel_strip[...], flat(do_r, N_COL * PAD)), opk)
-    o_out, o_in = gather(opk, o_r, q_peer, q_slot, ring, (1, 3, 2), o_send, o_recv)
-    for copy in o_out:
-        copy.start()
-    for o in (1, 3, 2):
+    for o in (0, 1, 3, 2):
         stats_part(stats_member(o))
 
     stats_chunk(LEN_A, LEN_B)

time: 79.9 us -> 78.8 us (0.986)
  Pallas kernels: 78.2 us -> 76.7 us
    pallas_call x1, Pallas kernels: 78.2 us -> 76.7 us  [shards(): pl.pallas_call(kernel, out_shape=jax.ShapeDtypeStruct((TILE * SAMPLES, C)...]
where the time goes in v5:
time: 78.8 us; the launch traced here: 78.2 us
  Pallas kernels  76.7 us (97%)
  local copies, waits for them, and re-layouts  1.52 us (2%)
    pallas_call x1, Pallas kernels, shards(): pl.pallas_call(kernel, out_shape=jax.ShapeDtypeStruct((TILE * SAMPLES, C)...  76.7 us

profile of v5, /device:TPU:1, one launch (start us, length us, event | category | flops | bytes accessed | tf_op | source)
XLA Modules:
  0.0 78.2 jit_solution(16113900384140358331)
XLA Ops:
  0.0 76.7 %shard_map.127 = bf16[144,256]{1,0:T(8,128)(2,1)} custom-call(bf16[3,6,8,256]{3,2,1,0:T(8,128)(2,1)} %bitcast.12, bf16[3,6,8,256]{3,2,1,0:T(8,128)(2,1)} %bitcast.13, bf16[2,64,288]{2,1,0:T(8,128)(2,1)} %bitcast.9, bf16[2,64,288]{2,1,0:T(8,128)(2,1)} %bitcast.10, bf16[2,64,288]{2,1,0:T(8,128)(2,1)} %bitcast.11, bf16[128,128]{1,0:T(8,128)(2,1)} %constant.14.clone.eye, ...), custom_call_target="tpu_custom_call" | custom-call | tf_op jit(solution)/shard_map/pallas_call | solution.py:490
  76.7 1.5 %copy.15 = bf16[8,3,6,256]{3,0,2,1:T(8,128)(2,1)} copy(bf16[8,3,6,256]{3,0,2,1:T(8,128)(2,1)} %bitcast.8) | data formatting | bytes 147456

commit v6 on v5

--- a/solution.py
+++ b/solution.py
@@ -51,7 +51,14 @@
             for half in range(2):
                 back[n * MSG + half * TILE + t, half * STRIP + place] = 1.0
                 got[half * TILE * SAMPLES + row, n * MSG + half * TILE + t] = 1.0
-    return tile, strip, back, got
+    row_back = np.zeros((N_COL * 8, PART_B), np.float32)
+    row_got = np.zeros((TC * SAMPLES, SAMPLES * 8), np.float32)
+    for t in range(TC):
+        for n in range(N_COL):
+            row_back[n * 8 + t, n * TC + t] = 1.0
+        for s in range(SAMPLES):
+            row_got[t * SAMPLES + s, s * 8 + t] = 1.0
+    return tile, strip, back, got, row_back, row_got
 
 
 def dot(a, b):
@@ -60,10 +67,6 @@
 
 def dot_nt(a, b):
     return lax.dot_general(a, b, NT, preferred_element_type=F32)
-
-
-def dot_tn(a, b):
-    return lax.dot_general(a, b, (((0,), (0,)), ((), ())), preferred_element_type=F32)
 
 
 def swap(x):
@@ -74,9 +77,9 @@
     og, zz, qh, kh, vh, eye, *refs,
 ):
     (
-        hbm_cw, hbm_ow, hbm_iw, hbm_tile, hbm_strip, hbm_back, hbm_got,
+        hbm_cw, hbm_ow, hbm_iw, hbm_tile, hbm_strip, hbm_back, hbm_got, hbm_row_back, hbm_row_got,
         out,
-        cw, ow, iw, sel_tile, sel_strip, sel_back, sel_got, load_sem,
+        cw, ow, iw, sel_tile, sel_strip, sel_back, sel_got, row_back, row_got, load_sem,
         xp, gz_keep, ga_s, do_r, qpk, opk, kvpk, q_r, o_r, kv_r, qz, oz, k_t, v_t1,
         o_t, e_s, st_s, lse_s, lse_r, rd_s, rd_r, kv_acc, kvo, kv_part, dq_t, qa, qb,
         qa_part, qb_part, g_s, g_r, h_s, h_r,
@@ -90,7 +93,8 @@
         pltpu.make_async_copy(src, dst, load_sem.at[n])
         for n, (src, dst) in enumerate(
             [(hbm_cw, cw), (hbm_tile, sel_tile), (hbm_ow, ow), (hbm_strip, sel_strip),
-             (hbm_iw, iw), (hbm_back, sel_back), (hbm_got, sel_got)]
+             (hbm_iw, iw), (hbm_back, sel_back), (hbm_got, sel_got),
+             (hbm_row_back, row_back), (hbm_row_got, row_got)]
         )
     ]
     core = lax.rem(r, 2)
@@ -437,22 +441,23 @@
     def weight(kind):
         return iw[:, pl.ds(pl.multiple_of(kind * C + lax.rem(c, 2) * 128, 128), 128)]
 
-    projected = (dot_nt(dk, weight(1)) + dot_nt(dv, weight(2))).astype(BF)
+    def unpacked(part, keep):
+        q0, q1 = [sum(part[p, n].astype(F32) for n in range(4)) for p in range(2)]
+        both = [jnp.where(keep, q0, swap(q1)), jnp.where(keep, swap(q0), q1)]
+        return jnp.concatenate(both, axis=0).astype(BF)
+
+    arrive(qa.at[0], qa_part, d_send, d_recv, q_peer)
+    projected = dot_nt(dk, weight(1)) + dot_nt(dv, weight(2))
+    first = projected[:PART_A] + dot_nt(unpacked(qa_part, lanes[:HALF_A]), weight(0))
+    projected = jnp.concatenate([first, projected[PART_A:]], axis=0).astype(BF)
     projected = jnp.concatenate([projected[:, :128], projected[:, 128:]], axis=0)
     placed = dot(sel_back[...], projected)
     g_s[...] = placed.reshape(N_COL, MSG // 8, 8, 128).astype(BF)
     b_out, b_in = exchange(g_s, g_r, b_send, b_recv)
 
-    arrive(qa.at[0], qa_part, d_send, d_recv, q_peer)
     arrive(qb.at[0], qb_part, e_send, e_recv, q_peer)
-
-    def unpacked(part, keep):
-        q0, q1 = [sum(part[p, n].astype(F32) for n in range(4)) for p in range(2)]
-        return [jnp.where(keep, q0, swap(q1)), jnp.where(keep, swap(q0), q1)]
-
-    dq = unpacked(qa_part, lanes[:HALF_A]) + unpacked(qb_part, lanes[:HALF_B])
-    placed = dot_tn(sel_strip[...], jnp.concatenate(dq, axis=0).astype(BF))
-    h_s[...] = placed.reshape(N_COL, PAD // 8, 8, 128).astype(BF)
+    placed = dot(row_back[...], unpacked(qb_part, lanes[:HALF_B]))
+    h_s[...] = placed.reshape(N_COL, 8, 128).astype(BF)
     h_out, h_in = exchange(h_s, h_r, h_send, h_recv)
     rows = TILE * SAMPLES
     for copy in b_in:
@@ -461,10 +466,12 @@
     total = gz_keep[...] + jnp.concatenate([sums[:rows], sums[rows:]], axis=1)
     for copy in h_in:
         copy.wait_recv()
+    late = total[(TR - 1) * TC * SAMPLES :]
     for b in range(2):
         got = jnp.concatenate([h_r[2 * s + b].astype(F32) for s in range(SAMPLES)], axis=0)
-        got = dot_tn(sel_tile[...], got.reshape(SAMPLES * PAD, 128).astype(BF)).astype(BF)
-        total = total + dot_nt(got, iw[:, b * 128 : (b + 1) * 128])
+        got = dot(row_got[...], got.astype(BF)).astype(BF)
+        late = late + dot_nt(got, iw[:, b * 128 : (b + 1) * 128])
+    total = jnp.concatenate([total[: (TR - 1) * TC * SAMPLES], late], axis=0)
     out[...] = total.astype(BF)
 
     for copy in halos + kv_out + q_out + a_out + o_out + l_out + t_out + b_out + h_out:
@@ -490,11 +497,11 @@
     result = pl.pallas_call(
         kernel,
         out_shape=jax.ShapeDtypeStruct((TILE * SAMPLES, C), BF),
-        in_specs=[vmem] * 6 + [pl.BlockSpec(memory_space=pl.ANY)] * 7,
+        in_specs=[vmem] * 6 + [pl.BlockSpec(memory_space=pl.ANY)] * 9,
         out_specs=vmem,
         scratch_shapes=[
             *[pltpu.VMEM(x.shape, BF) for x in (conv_weight, out_weight, input_weight, *sel)],
-            dma(7),
+            dma(9),
             pltpu.VMEM((TR + 2, TC + 2, SAMPLES, C), BF),
             pltpu.VMEM((TILE * SAMPLES, C), F32),
             pltpu.VMEM((N_COL, PAD // 8, 8, 128), BF),
@@ -526,8 +533,8 @@
             pltpu.VMEM((2, 4, HALF_B, 128), BF),
             pltpu.VMEM((N_COL, MSG // 8, 8, 128), BF),
             pltpu.VMEM((N_COL, MSG // 8, 8, 128), BF),
-            pltpu.VMEM((N_COL, PAD // 8, 8, 128), BF),
-            pltpu.VMEM((N_COL, PAD // 8, 8, 128), BF),
+            pltpu.VMEM((N_COL, 8, 128), BF),
+            pltpu.VMEM((N_COL, 8, 128), BF),
             dma(8), dma(8), dma(16), dma(16), dma(8), dma(8), dma(8), dma(8),
             dma(8), dma(8), dma(4), dma(4), dma(4), dma(4), dma(8), dma(2, 4), dma(8), dma(2, 4),
             dma(8), dma(2, 4), dma(16), dma(16), dma(16), dma(16),

time: 78.8 us -> 78.3 us (level)
  no operation moved by 1% of the time
where the time goes in v6:
time: 78.3 us; the launch traced here: 78.2 us
  Pallas kernels  76.6 us (98%)
  local copies, waits for them, and re-layouts  1.52 us (2%)
    pallas_call x1, Pallas kernels, shards(): pl.pallas_call(kernel, out_shape=jax.ShapeDtypeStruct((TILE * SAMPLES, C)...  76.6 us

profile of v6, /device:TPU:1, one launch (start us, length us, event | category | flops | bytes accessed | tf_op | source)
XLA Modules:
  0.0 78.2 jit_solution(6467620629606692228)
XLA Ops:
  0.0 76.6 %shard_map.145 = bf16[144,256]{1,0:T(8,128)(2,1)} custom-call(bf16[3,6,8,256]{3,2,1,0:T(8,128)(2,1)} %bitcast.12, bf16[3,6,8,256]{3,2,1,0:T(8,128)(2,1)} %bitcast.13, bf16[2,64,288]{2,1,0:T(8,128)(2,1)} %bitcast.9, bf16[2,64,288]{2,1,0:T(8,128)(2,1)} %bitcast.10, bf16[2,64,288]{2,1,0:T(8,128)(2,1)} %bitcast.11, bf16[128,128]{1,0:T(8,128)(2,1)} %constant.20.clone.eye, ...), custom_call_target="tpu_custom_call" | custom-call | tf_op jit(solution)/shard_map/pallas_call | solution.py:497
  76.6 1.5 %copy.17 = bf16[8,3,6,256]{3,0,2,1:T(8,128)(2,1)} copy(bf16[8,3,6,256]{3,0,2,1:T(8,128)(2,1)} %bitcast.8) | data formatting | bytes 147456

commit v7 on v6

--- a/solution.py
+++ b/solution.py
@@ -329,6 +329,14 @@
     for o in (0, 1, 3, 2):
         stats_part(stats_member(o))
 
+    def cotangents(o):
+        for copy in o_in[o]:
+            copy.wait_recv()
+        for k in range(2):
+            unpack(o_r, q_slot(o) * 2 + k, oz, False)
+
+    for o in (0, 1, 3):
+        cotangents(o)
     stats_chunk(LEN_A, LEN_B)
 
     def share(src, dst, send, recv):
@@ -344,11 +352,7 @@
 
     lse_s[...] = st_s[0:1] + jnp.log(st_s[1:2]) * LOG2E
     l_out, l_in = share(lse_s, lse_r, l_send, l_recv)
-    for o in range(4):
-        for copy in o_in[o]:
-            copy.wait_recv()
-    for k in range(8):
-        unpack(o_r, k, oz, False)
+    cotangents(2)
     do_t = dot_nt(eye[64:], oz[...])
     rd_s[...] = jnp.sum(o_t[...] * do_t, axis=0, keepdims=True) / st_s[2:3]
     t_out, t_in = share(rd_s, rd_r, t_send, t_recv)

time: 78.3 us -> 80.7 us (1.031)
  Pallas kernels: 76.6 us -> 78.9 us
    pallas_call x1, Pallas kernels: 76.6 us -> 78.9 us  [shards(): pl.pallas_call(kernel, out_shape=jax.ShapeDtypeStruct((TILE * SAMPLES, C)...]
where the time goes in v7:
time: 80.7 us; the launch traced here: 80.5 us
  Pallas kernels  78.9 us (98%)
  local copies, waits for them, and re-layouts  1.52 us (2%)
    pallas_call x1, Pallas kernels, shards(): pl.pallas_call(kernel, out_shape=jax.ShapeDtypeStruct((TILE * SAMPLES, C)...  78.9 us

profile of v7, /device:TPU:1, one launch (start us, length us, event | category | flops | bytes accessed | tf_op | source)
XLA Modules:
  0.0 80.5 jit_solution(4028490537643499524)
XLA Ops:
  0.0 78.9 %shard_map.145 = bf16[144,256]{1,0:T(8,128)(2,1)} custom-call(bf16[3,6,8,256]{3,2,1,0:T(8,128)(2,1)} %bitcast.12, bf16[3,6,8,256]{3,2,1,0:T(8,128)(2,1)} %bitcast.13, bf16[2,64,288]{2,1,0:T(8,128)(2,1)} %bitcast.9, bf16[2,64,288]{2,1,0:T(8,128)(2,1)} %bitcast.10, bf16[2,64,288]{2,1,0:T(8,128)(2,1)} %bitcast.11, bf16[128,128]{1,0:T(8,128)(2,1)} %constant.20.clone.eye, ...), custom_call_target="tpu_custom_call" | custom-call | tf_op jit(solution)/shard_map/pallas_call | solution.py:501
  78.9 1.5 %copy.17 = bf16[8,3,6,256]{3,0,2,1:T(8,128)(2,1)} copy(bf16[8,3,6,256]{3,0,2,1:T(8,128)(2,1)} %bitcast.8) | data formatting | bytes 147456
